TPU v7x, 256 devices: a whole 4x4x8 slice. The times are simulated.
256 devices in a mesh: dom: 64 (over z, x, core), sub: 4 (over y).
Axes of the slice: x: 4, y: 4, z: 8, core: 2. Of those that a mesh axis runs over, the one named last changes fastest.
Arguments:
- source: float32 [32, 1024, 512], P(None, 'dom', 'sub'), may hold values from -100 to 100
- initial: float32 [32, 1024, 512], P(None, 'dom', 'sub'), may hold values from -6 to 6
- lumped_mass: float32 [1024, 512], P('dom', 'sub'), may hold values from 0.25 to 2.5
- node_slots: int32 [6, 1024, 512], P(None, 'dom', 'sub'), may hold values from 0 to 8, as said below
- stiffness: float32 [6, 6, 1024, 512], P(None, None, 'dom', 'sub'), as said below
Outputs:
- new_residual: float32 [32, 1024, 512], P(None, 'dom', 'sub')
- upper_factor: float32 [128, 128], replicated
Inputs may be any that keep to these rules, and one draw needn't show every extreme that they name: `node_slots`: the six entries of one element are distinct offsets. `stiffness`: each 6 x 6 element matrix is symmetric and diagonally dominant.
All inputs are finite; a program needn't handle non-finite values.
Results may differ from a plain program's by a relative error of at most 0.012.
Values sent between devices are 32-bit elements; how exact they have to be, the bound alone decides.
No kernel may reach another device: no remote copies, remote signals or barrier semaphores. Data moves between devices by JAX's collectives and lax.ppermute only.
A program may use at most 64 MiB of HBM per device.

v0:
```python
import jax
import jax.numpy as jnp
from jax import lax
from jax.sharding import PartitionSpec as P

STEPS = 4


def padded(cells, sides, width):
    for axis, dim in sides:
        count = lax.axis_size(axis)
        ends = count - 1
        head = lax.slice_in_dim(cells, 0, width, axis=dim)
        tail = lax.slice_in_dim(cells, cells.shape[dim] - width, cells.shape[dim], axis=dim)
        cells = jnp.concatenate(
            [
                lax.ppermute(tail, axis, [(i, (i + 1) % count) for i in range(ends)]),
                cells,
                lax.ppermute(head, axis, [((i + 1) % count, i) for i in range(ends)]),
            ],
            axis=dim,
        )
    return cells


def passed_along(value, axis, steps):
    count = lax.axis_size(axis)
    first, last = (max(0, -steps), min(count, count - steps))
    return lax.ppermute(value, axis, [(source, source + steps) for source in range(first, last)])


def offset_matrix(node_slots, stiffness):
    result = []
    middle = []
    for target in range(9):
        acc = jnp.zeros(stiffness.shape[1:], jnp.float32)
        for second in range(6):
            acc = (
                acc
                + stiffness[:, second] * (node_slots[second] == target).astype(jnp.float32)[None]
            )
        middle.append(acc)
    for first_off in range(9):
        for second_off in range(9):
            value = jnp.sum(
                middle[second_off] * (node_slots == first_off).astype(jnp.float32), axis=0
            )
            result.append(value)
    return jnp.stack(result, axis=0)


def on_device(source, initial, lumped_mass, node_slots, stiffness):
    height, breadth = lumped_mass.shape
    nfield = source.shape[0]
    coeffs = offset_matrix(node_slots, stiffness)

    def apply(field):
        ghost = padded(field, (("dom", 1), ("sub", 2)), 1)
        gathered = []
        for second_off in range(9):
            row_q = second_off // 3 - 1
            col_q = second_off % 3 - 1
            gathered.append(
                ghost[:, 1 + row_q : 1 + row_q + height, 1 + col_q : 1 + col_q + breadth]
            )
        accum = jnp.zeros(ghost.shape, jnp.float32)
        for first_off in range(9):
            row_p = first_off // 3 - 1
            col_p = first_off % 3 - 1
            partial_sum = coeffs[first_off * 9][None] * gathered[0]
            for second_off in range(1, 9):
                partial_sum = (
                    partial_sum + coeffs[first_off * 9 + second_off][None] * gathered[second_off]
                )
            accum = accum.at[
                :, 1 + row_p : 1 + row_p + height, 1 + col_p : 1 + col_p + breadth
            ].add(partial_sum)
        from_above = passed_along(accum[:, height + 1, :], "dom", 1)
        from_below = passed_along(accum[:, 0, :], "dom", -1)
        accum = accum.at[:, 1, :].add(from_above).at[:, height, :].add(from_below)
        inner = accum[:, 1 : height + 1, :]
        from_left = passed_along(inner[:, :, breadth + 1], "sub", 1)
        from_right = passed_along(inner[:, :, 0], "sub", -1)
        inner = inner.at[:, :, 1].add(from_left).at[:, :, breadth].add(from_right)
        return lumped_mass[None] * field + inner[:, :, 1 : breadth + 1]

    start_residual = source - apply(initial)
    previous = start_residual
    blocks = []
    for step in range(STEPS):
        image = apply(previous)
        blocks.append(image.reshape(nfield, height * breadth))
        if step + 1 < STEPS:
            previous = image - 2.0 * previous
    basis = jnp.concatenate(blocks, axis=0)
    flat = start_residual.reshape(nfield, height * breadth)
    count = float(height * breadth * lax.axis_size("dom") * lax.axis_size("sub"))
    gram_local = jnp.dot(basis, basis.T, precision=lax.Precision.HIGHEST) / count
    projected_local = jnp.dot(basis, flat.T, precision=lax.Precision.HIGHEST) / count
    gram, projected = lax.psum((gram_local, projected_local), ("dom", "sub"))
    lower = jnp.linalg.cholesky(gram)
    upper = lower.T
    solved = jax.scipy.linalg.cho_solve((lower, True), projected)
    new_flat = flat - jnp.dot(solved.T, basis, precision=lax.Precision.HIGHEST)
    return (new_flat.reshape(nfield, height, breadth), upper)


def solution(mesh):
    return jax.shard_map(
        on_device,
        mesh=mesh,
        in_specs=(
            P(None, "dom", "sub"),
            P(None, "dom", "sub"),
            P("dom", "sub"),
            P(None, "dom", "sub"),
            P(None, None, "dom", "sub"),
        ),
        out_specs=(P(None, "dom", "sub"), P()),
        check_vma=False,
    )
```

profile of v0, /device:TPU:1, one launch (start us, length us, event | category | flops | bytes accessed | tf_op | source)
XLA Modules:
  0.0 656.3 jit_solution(1628703541807910034)
XLA Ops:
  8.3 5.1 collective-permute-start.1
  21.2 4.0 collective-permute-start.2
  25.9 4.0 collective-permute-done.3
  34.7 4.1 scatter-add.219
  38.8 3.0 add_select_fusion.4
  41.7 4.1 scatter-add.220
  46.5 2.8 scatter-add.224
  49.7 2.8 scatter-add.225
  53.1 2.8 scatter-add.229
  56.3 2.8 scatter-add.230
  59.2 4.0 collective-permute-start.4
  66.1 3.9 collective-permute-done.5
  70.3 4.1 collective-permute-start.6
  81.7 3.3 collective-permute-start.8
  87.2 2.9 collective-permute-done.9
  90.2 3.2 collective-permute-start.10
  94.8 4.0 collective-permute-done.10
  98.8 4.1 collective-permute-done.11
  106.7 4.1 scatter-add.240
  110.8 3.0 add_select_fusion.3
  113.8 4.1 scatter-add.241
  118.7 2.8 scatter-add.245
  121.9 2.8 scatter-add.246
  125.5 2.8 scatter-add.250
  128.7 2.8 scatter-add.251
  131.6 4.3 collective-permute-start.12
  138.8 3.9 collective-permute-done.13
  143.0 3.2 collective-permute-start.14
  153.1 3.3 collective-permute-start.16
  158.4 3.1 collective-permute-done.17
  165.1 3.6 collective-permute-done.18
  168.7 4.1 collective-permute-done.19
  176.7 4.1 scatter-add.261
  180.9 3.0 add_select_fusion.2
  183.9 4.1 scatter-add.264
  188.9 2.8 scatter-add.266
  195.8 2.8 scatter-add.271
  199.0 2.8 scatter-add.274
  201.9 4.2 collective-permute-start.20
  209.1 3.9 collective-permute-done.21
  221.6 3.3 collective-permute-start.24
  226.9 3.1 collective-permute-done.25
  233.3 3.8 collective-permute-done.26
  237.1 4.1 collective-permute-done.27
  245.1 4.1 scatter-add.284
  249.1 3.1 add_select_fusion.1
  252.3 4.2 scatter-add.285
  264.9 2.8 scatter-add.294
  268.1 2.8 scatter-add.295
  271.0 4.2 collective-permute-start.28
  278.1 3.9 collective-permute-done.29
  291.1 3.3 collective-permute-start.32
  296.4 3.1 collective-permute-done.33
  302.9 3.8 collective-permute-done.34
  306.6 4.1 collective-permute-done.35
  314.6 4.1 scatter-add.305
  318.6 3.1 add_select_fusion
  321.7 4.1 scatter-add.306
  342.0 3.8 collective-permute-start.36
  348.8 3.9 collective-permute-done.37
  364.0 97.4 %psum.15 = f32[128,32]{0,1:T(8,128)S(1)} all-reduce(f32[128,32]{0,1:T(8,128)S(1)} %convolution_multiply_fusion.1), channel_id=1, replica_groups=mesh['dom'=64,'sub'=4] {'dom','sub'}, use_global_device_ids=true, to_apply=%region_85.0 | all-reduce | flops 4096 | bytes 32768 | tf_op jit(solution)/shard_map/psum | solution.py:100
  461.4 161.1 %all-reduce.7.cloned.1.call-done = f32[128,128]{0,1:T(8,128)} async-done(((f32[128,128]{0,1:T(8,128)}), f32[128,128]{0,1:T(8,128)}) %all-reduce.7.cloned.1.call-update) | async-done | bytes 65552 | tf_op jit(solution)/shard_map/psum | solution.py:100
  623.6 11.7 %cholesky.16 = f32[128,128]{1,0:T(8,128)S(1)} custom-call(f32[128,128]{1,0:T(8,128)S(1)} %fusion.26), custom_call_target="Cholesky" | custom-call | tf_op jit(solution)/shard_map/jit(cholesky)/cholesky | solution.py:101
  637.4 9.8 %custom-call.10 = f32[1,128,128]{1,2,0:T(8,128)S(1)} custom-call(f32[1,128,128]{2,1,0:T(8,128)S(1)} %get-tuple-element.1265), custom_call_target="InvertDiagBlocksLowerTriangular" | custom-call | tf_op jit(solution)/shard_map/jit(_cho_solve)/triangular_solve | solution.py:103
  (403 shorter events, 144.9 us)
Async XLA Ops:
  7.2 615.4 %all-reduce.7.cloned.1.call-start = ((), (), s32[]{:S(2)}) async-start(), calls=%async_computation | async-start | bytes 131072 | tf_op jit(solution)/shard_map/psum | solution.py:100
  8.3 11.5 %collective-permute-start.1 = (f32[32,1,128]{2,0,1:T(8,128)S(1)}, f32[32,1,128]{2,0,1:T(8,128)S(1)}, u32[]{:S(2)}, u32[]{:S(2)}) collective-permute-start(f32[32,1,128]{2,0,1:T(8,128)S(1)} %get-tuple-element.1262), channel_id=1, source_target_pairs={{4,0},{8,4},{12,8},{16,12},{20,16},{24,20},{28,24},{32,28},{36,32}... | collective-permute-start | bytes 49160 | tf_op jit(solution)/shard_map/ppermute | solution.py:19
  13.4 6.2 collective-permute-start
  18.8 169.6 %copy-start.30 = (f32[16,128]{1,0:T(8,128)}, f32[16,128]{1,0:T(8,128)S(1)}, u32[]{:S(2)}) copy-start(f32[16,128]{1,0:T(8,128)S(1)} %get-tuple-element.1140) | copy-start | bytes 24580
  18.8 169.6 %copy-start.33 = (f32[16,128]{1,0:T(8,128)}, f32[16,128]{1,0:T(8,128)S(1)}, u32[]{:S(2)}) copy-start(f32[16,128]{1,0:T(8,128)S(1)} %get-tuple-element.1149) | copy-start | bytes 24580
  18.8 169.6 %copy-start.36 = (f32[16,128]{1,0:T(8,128)}, f32[16,128]{1,0:T(8,128)S(1)}, u32[]{:S(2)}) copy-start(f32[16,128]{1,0:T(8,128)S(1)} %get-tuple-element.1158) | copy-start | bytes 24580
  18.8 169.6 %copy-start.39 = (f32[16,128]{1,0:T(8,128)}, f32[16,128]{1,0:T(8,128)S(1)}, u32[]{:S(2)}) copy-start(f32[16,128]{1,0:T(8,128)S(1)} %get-tuple-element.1167) | copy-start | bytes 24580
  18.8 169.6 %copy-start.42 = (f32[16,128]{1,0:T(8,128)}, f32[16,128]{1,0:T(8,128)S(1)}, u32[]{:S(2)}) copy-start(f32[16,128]{1,0:T(8,128)S(1)} %get-tuple-element.1172) | copy-start | bytes 24580
  18.8 169.6 %copy-start.45 = (f32[16,128]{1,0:T(8,128)}, f32[16,128]{1,0:T(8,128)S(1)}, u32[]{:S(2)}) copy-start(f32[16,128]{1,0:T(8,128)S(1)} %get-tuple-element.1181) | copy-start | bytes 24580
  18.8 169.6 %copy-start.48 = (f32[16,128]{1,0:T(8,128)}, f32[16,128]{1,0:T(8,128)S(1)}, u32[]{:S(2)}) copy-start(f32[16,128]{1,0:T(8,128)S(1)} %get-tuple-element.1190) | copy-start | bytes 24580
  18.8 169.6 %copy-start.51 = (f32[16,128]{1,0:T(8,128)}, f32[16,128]{1,0:T(8,128)S(1)}, u32[]{:S(2)}) copy-start(f32[16,128]{1,0:T(8,128)S(1)} %get-tuple-element.1199) | copy-start | bytes 24580
  18.8 169.6 %copy-start.54 = (f32[16,128]{1,0:T(8,128)}, f32[16,128]{1,0:T(8,128)S(1)}, u32[]{:S(2)}) copy-start(f32[16,128]{1,0:T(8,128)S(1)} %get-tuple-element.1208) | copy-start | bytes 24580
  18.9 172.9 %copy-start.12 = (f32[16,128]{1,0:T(8,128)}, f32[16,128]{1,0:T(8,128)S(1)}, u32[]{:S(2)}) copy-start(f32[16,128]{1,0:T(8,128)S(1)} %get-tuple-element.1135) | copy-start | bytes 24580
  18.9 172.9 %copy-start.14 = (f32[16,128]{1,0:T(8,128)}, f32[16,128]{1,0:T(8,128)S(1)}, u32[]{:S(2)}) copy-start(f32[16,128]{1,0:T(8,128)S(1)} %get-tuple-element.1144) | copy-start | bytes 24580
  18.9 172.9 %copy-start.16 = (f32[16,128]{1,0:T(8,128)}, f32[16,128]{1,0:T(8,128)S(1)}, u32[]{:S(2)}) copy-start(f32[16,128]{1,0:T(8,128)S(1)} %get-tuple-element.1153) | copy-start | bytes 24580
  18.9 172.9 %copy-start.18 = (f32[16,128]{1,0:T(8,128)}, f32[16,128]{1,0:T(8,128)S(1)}, u32[]{:S(2)}) copy-start(f32[16,128]{1,0:T(8,128)S(1)} %get-tuple-element.1162) | copy-start | bytes 24580
  18.9 172.9 %copy-start.20 = (f32[16,128]{1,0:T(8,128)}, f32[16,128]{1,0:T(8,128)S(1)}, u32[]{:S(2)}) copy-start(f32[16,128]{1,0:T(8,128)S(1)} %get-tuple-element.1171) | copy-start | bytes 24580
  18.9 172.9 %copy-start.22 = (f32[16,128]{1,0:T(8,128)}, f32[16,128]{1,0:T(8,128)S(1)}, u32[]{:S(2)}) copy-start(f32[16,128]{1,0:T(8,128)S(1)} %get-tuple-element.1177) | copy-start | bytes 24580
  18.9 172.9 %copy-start.24 = (f32[16,128]{1,0:T(8,128)}, f32[16,128]{1,0:T(8,128)S(1)}, u32[]{:S(2)}) copy-start(f32[16,128]{1,0:T(8,128)S(1)} %get-tuple-element.1186) | copy-start | bytes 24580
  18.9 172.9 %copy-start.26 = (f32[16,128]{1,0:T(8,128)}, f32[16,128]{1,0:T(8,128)S(1)}, u32[]{:S(2)}) copy-start(f32[16,128]{1,0:T(8,128)S(1)} %get-tuple-element.1195) | copy-start | bytes 24580
  18.9 172.9 %copy-start.28 = (f32[16,128]{1,0:T(8,128)}, f32[16,128]{1,0:T(8,128)S(1)}, u32[]{:S(2)}) copy-start(f32[16,128]{1,0:T(8,128)S(1)} %get-tuple-element.1204) | copy-start | bytes 24580
  18.9 176.1 %copy-start.2 = (f32[16,128]{1,0:T(8,128)}, f32[16,128]{1,0:T(8,128)S(1)}, u32[]{:S(2)}) copy-start(f32[16,128]{1,0:T(8,128)S(1)} %get-tuple-element.1170) | copy-start | bytes 24580
  19.0 176.1 %copy-start.4 = (f32[16,128]{1,0:T(8,128)}, f32[16,128]{1,0:T(8,128)S(1)}, u32[]{:S(2)}) copy-start(f32[16,128]{1,0:T(8,128)S(1)} %get-tuple-element.1178) | copy-start | bytes 24580
  19.0 176.1 %copy-start.6 = (f32[16,128]{1,0:T(8,128)}, f32[16,128]{1,0:T(8,128)S(1)}, u32[]{:S(2)}) copy-start(f32[16,128]{1,0:T(8,128)S(1)} %get-tuple-element.1187) | copy-start | bytes 24580
  19.0 176.1 %copy-start.8 = (f32[16,128]{1,0:T(8,128)}, f32[16,128]{1,0:T(8,128)S(1)}, u32[]{:S(2)}) copy-start(f32[16,128]{1,0:T(8,128)S(1)} %get-tuple-element.1196) | copy-start | bytes 24580
  19.0 176.1 %copy-start.10 = (f32[16,128]{1,0:T(8,128)}, f32[16,128]{1,0:T(8,128)S(1)}, u32[]{:S(2)}) copy-start(f32[16,128]{1,0:T(8,128)S(1)} %get-tuple-element.1205) | copy-start | bytes 24580
  19.9 10.0 %collective-permute-start.3 = (f32[32,18,1]{2,0,1:T(8,128)S(1)}, f32[32,18,1]{2,0,1:T(8,128)S(1)}, u32[]{:S(2)}, u32[]{:S(2)}) collective-permute-start(f32[32,18,1]{2,0,1:T(8,128)S(1)} %get-tuple-element.1252), channel_id=1, source_target_pairs={{1,0},{2,1},{3,2},{5,4},{6,5},{7,6},{9,8},{10,9},{11,10},{13,12},{... | collective-permute-start | bytes 6920 | tf_op jit(solution)/shard_map/ppermute | solution.py:19
  21.2 9.6 %collective-permute-start.2 = (f32[32,18,1]{2,0,1:T(8,128)S(1)}, f32[32,18,1]{2,0,1:T(8,128)S(1)}, u32[]{:S(2)}, u32[]{:S(2)}) collective-permute-start(f32[32,18,1]{2,0,1:T(8,128)S(1)} %get-tuple-element.1253), channel_id=1, source_target_pairs={{0,1},{1,2},{2,3},{4,5},{5,6},{6,7},{8,9},{9,10},{10,11},{12,13},{... | collective-permute-start | bytes 6920 | tf_op jit(solution)/shard_map/ppermute | solution.py:17
  59.2 5.0 collective-permute-start.4
  64.2 5.8 collective-permute-start.5
  70.3 5.5 collective-permute-start.6
  74.5 4.4 collective-permute-start.7
  81.7 5.5 collective-permute-start.8
  85.0 5.1 collective-permute-start.9
  90.2 8.5 %collective-permute-start.10 = (f32[32,18,1]{2,0,1:T(8,128)S(1)}, f32[32,18,1]{2,0,1:T(8,128)S(1)}, u32[]{:S(2)}, u32[]{:S(2)}) collective-permute-start(f32[32,18,1]{2,0,1:T(8,128)S(1)} %get-tuple-element.1250), channel_id=1, source_target_pairs={{0,1},{1,2},{2,3},{4,5},{5,6},{6,7},{8,9},{9,10},{10,11},{12,13},{... | collective-permute-start | bytes 6920 | tf_op jit(solution)/shard_map/ppermute | solution.py:17
  93.5 9.4 %collective-permute-start.11 = (f32[32,18,1]{2,0,1:T(8,128)S(1)}, f32[32,18,1]{2,0,1:T(8,128)S(1)}, u32[]{:S(2)}, u32[]{:S(2)}) collective-permute-start(f32[32,18,1]{2,0,1:T(8,128)S(1)} %get-tuple-element.1251), channel_id=1, source_target_pairs={{1,0},{2,1},{3,2},{5,4},{6,5},{7,6},{9,8},{10,9},{11,10},{13,12},{... | collective-permute-start | bytes 6920 | tf_op jit(solution)/shard_map/ppermute | solution.py:19
  131.6 5.3 collective-permute-start.12
  136.9 5.8 collective-permute-start.13
  143.0 4.6 collective-permute-start.14
  146.3 4.4 collective-permute-start.15
  153.1 5.3 collective-permute-start.16
  156.5 5.1 collective-permute-start.17
  161.7 7.0 %collective-permute-start.18 = (f32[32,18,1]{2,0,1:T(8,128)S(1)}, f32[32,18,1]{2,0,1:T(8,128)S(1)}, u32[]{:S(2)}, u32[]{:S(2)}) collective-permute-start(f32[32,18,1]{2,0,1:T(8,128)S(1)} %get-tuple-element.1246), channel_id=1, source_target_pairs={{0,1},{1,2},{2,3},{4,5},{5,6},{6,7},{8,9},{9,10},{10,11},{12,13},{... | collective-permute-start | bytes 6920 | tf_op jit(solution)/shard_map/ppermute | solution.py:17
  163.4 9.4 %collective-permute-start.19 = (f32[32,18,1]{2,0,1:T(8,128)S(1)}, f32[32,18,1]{2,0,1:T(8,128)S(1)}, u32[]{:S(2)}, u32[]{:S(2)}) collective-permute-start(f32[32,18,1]{2,0,1:T(8,128)S(1)} %get-tuple-element.1247), channel_id=1, source_target_pairs={{1,0},{2,1},{3,2},{5,4},{6,5},{7,6},{9,8},{10,9},{11,10},{13,12},{... | collective-permute-start | bytes 6920 | tf_op jit(solution)/shard_map/ppermute | solution.py:19
  201.9 5.2 collective-permute-start.20
  207.1 5.8 collective-permute-start.21
  213.3 3.3 collective-permute-start.22
  215.2 4.4 collective-permute-start.23
  221.6 5.3 collective-permute-start.24
  225.0 5.1 collective-permute-start.25
  230.2 7.0 %collective-permute-start.26 = (f32[32,18,1]{2,0,1:T(8,128)S(1)}, f32[32,18,1]{2,0,1:T(8,128)S(1)}, u32[]{:S(2)}, u32[]{:S(2)}) collective-permute-start(f32[32,18,1]{2,0,1:T(8,128)S(1)} %get-tuple-element.1242), channel_id=1, source_target_pairs={{0,1},{1,2},{2,3},{4,5},{5,6},{6,7},{8,9},{9,10},{10,11},{12,13},{... | collective-permute-start | bytes 6920 | tf_op jit(solution)/shard_map/ppermute | solution.py:17
  231.9 9.4 %collective-permute-start.27 = (f32[32,18,1]{2,0,1:T(8,128)S(1)}, f32[32,18,1]{2,0,1:T(8,128)S(1)}, u32[]{:S(2)}, u32[]{:S(2)}) collective-permute-start(f32[32,18,1]{2,0,1:T(8,128)S(1)} %get-tuple-element.1243), channel_id=1, source_target_pairs={{1,0},{2,1},{3,2},{5,4},{6,5},{7,6},{9,8},{10,9},{11,10},{13,12},{... | collective-permute-start | bytes 6920 | tf_op jit(solution)/shard_map/ppermute | solution.py:19
  271.0 5.2 collective-permute-start.28
  276.2 5.8 collective-permute-start.29
  282.3 3.3 collective-permute-start.30
  284.2 4.4 collective-permute-start.31
  291.1 5.3 collective-permute-start.32
  294.4 5.1 collective-permute-start.33
  299.7 7.0 %collective-permute-start.34 = (f32[32,18,1]{2,0,1:T(8,128)S(1)}, f32[32,18,1]{2,0,1:T(8,128)S(1)}, u32[]{:S(2)}, u32[]{:S(2)}) collective-permute-start(f32[32,18,1]{2,0,1:T(8,128)S(1)} %get-tuple-element.1238), channel_id=1, source_target_pairs={{0,1},{1,2},{2,3},{4,5},{5,6},{6,7},{8,9},{9,10},{10,11},{12,13},{... | collective-permute-start | bytes 6920 | tf_op jit(solution)/shard_map/ppermute | solution.py:17
  301.3 9.4 %collective-permute-start.35 = (f32[32,18,1]{2,0,1:T(8,128)S(1)}, f32[32,18,1]{2,0,1:T(8,128)S(1)}, u32[]{:S(2)}, u32[]{:S(2)}) collective-permute-start(f32[32,18,1]{2,0,1:T(8,128)S(1)} %get-tuple-element.1239), channel_id=1, source_target_pairs={{1,0},{2,1},{3,2},{5,4},{6,5},{7,6},{9,8},{10,9},{11,10},{13,12},{... | collective-permute-start | bytes 6920 | tf_op jit(solution)/shard_map/ppermute | solution.py:19
  342.0 4.8 collective-permute-start.36
  346.9 5.8 collective-permute-start.37
  353.0 2.7 collective-permute-start.38
  354.4 4.4 collective-permute-start.39
  (74 other events, 2312.1 us)
Sparse Core Ops, SparseCore 0:
  363.0 259.5 all-reduce.6
where the time goes:
time: 668 us; the launch traced here: 656 us
  waiting for transfers between devices  248 us (37%)
  local copies, waits for them, and re-layouts  119 us (18%)
  blocking collectives  97.4 us (15%)
  starting transfers between devices  96.8 us (14%)
  other arithmetic  74 us (11%)
  between operations  17.4 us (3%)
    psum x1, waiting for transfers between devices, on_device(): gram, projected = lax.psum((gram_local, projected_local), ('dom', 'sub'))  161 us
    scatter-add x35, local copies, waits for them, and re-layouts, apply(): accum = accum.at[:, 1 + row_p:1 + row_p + height, 1 + col_p:1 + col_p + b...  98.1 us
    psum x1, blocking collectives, on_device(): gram, projected = lax.psum((gram_local, projected_local), ('dom', 'sub'))  97.4 us
    ppermute x20, starting transfers between devices, passed_along(): lax.ppermute(value, axis, [(source, source + steps) for source in range(f...  49 us
    ppermute x20, waiting for transfers between devices, passed_along(): lax.ppermute(value, axis, [(source, source + steps) for source in range(f...  38.2 us
    ppermute x10, waiting for transfers between devices, padded(): lax.ppermute(head, axis, [((i + 1) % count, i) for i in range(ends)])  32.7 us
    ppermute x10, starting transfers between devices, padded(): lax.ppermute(tail, axis, [(i, (i + 1) % count) for i in range(ends)])  27.5 us
    ppermute x10, starting transfers between devices, padded(): lax.ppermute(head, axis, [((i + 1) % count, i) for i in range(ends)])  20.3 us
  transfers between devices with their start and end apart: 41, of which 30 were waited for; matrix products, arithmetic and copies ran while one was open for 1% of the time, Pallas kernels for 0%

commit v1 on v0

v1 whole, which is shorter than its diff:
```python
import jax
import jax.numpy as jnp
import numpy as np
from jax import lax
from jax.experimental import pallas as pl
from jax.experimental.pallas import tpu as pltpu
from jax.sharding import Mesh, PartitionSpec as P

STEPS = 4
NF = 32
NR = 16
NC = 128
HALO = 10
INTERPRET = False
F32 = jnp.float32

HALF = [(0, 0), (0, 1), (0, 2)] + [(dr, dc) for dr in (1, 2) for dc in range(-2, 3)]
HALF_INDEX = {d: i for i, d in enumerate(HALF)}
NH = len(HALF)
TURNED = [d for d in HALF if d[1] != 0]
TURNED_INDEX = {d: NH + i for i, d in enumerate(TURNED)}
NCOEF = NH + len(TURNED)


def lanes(shape):
    return lax.broadcasted_iota(jnp.int32, shape, len(shape) - 1)


def turn(value, shift):
    shift = shift % NC
    return value if shift == 0 else pltpu.roll(value, shift, value.ndim - 1)


def call(body, outs, scratch=(), **kw):
    return pl.pallas_call(
        body,
        out_shape=outs,
        scratch_shapes=scratch,
        interpret=INTERPRET,
        **kw,
    )


def vmem_specs(count):
    return [pl.BlockSpec(memory_space=pltpu.VMEM)] * count


def prepare_body(rows_total, cols_total, pos, source, initial, mass, slots, stiffness,
                 ini_x, src_x, w_main, w_strip, to_left, to_right, acc):
    row = lax.broadcasted_iota(jnp.int32, (NR, NC), 0) + pos[0] * NR
    col = lanes((NR, NC)) + pos[1] * NC
    top, bottom = row == 0, row == rows_total - 1
    west, east = col == 0, col == cols_total - 1
    kept = []
    for a in range(6):
        slot = slots[a]
        in_west = (slot == 0) | (slot == 3) | (slot == 6)
        in_east = (slot == 2) | (slot == 5) | (slot == 8)
        outside = (top & (slot < 3)) | (bottom & (slot > 5)) | (west & in_west) | (east & in_east)
        kept.append(jnp.where(outside, 99, slot))
    acc[...] = jnp.zeros(acc.shape, F32)
    zero = jnp.zeros((NR, NC), F32)
    for q in range(9):
        middle = []
        for a in range(6):
            value = zero
            for b in range(6):
                value = jnp.where(kept[b] == q, stiffness[a * 6 + b], value)
            middle.append(value)
        for p in range(q + 1):
            value = zero
            for a in range(6):
                value = jnp.where(kept[a] == p, middle[a], value)
            place = HALF_INDEX[(q // 3 - p // 3, q % 3 - p % 3)]
            start = 7 + p // 3 - 1
            acc[p % 3, place, start:start + NR, :] += value
    acc[1, 0, 7:7 + NR, :] += mass[...]

    lane = lanes((24, NC))
    pack_left = [jnp.zeros((24, NC), F32) for _ in range(2)]
    pack_right = [jnp.zeros((24, NC), F32) for _ in range(2)]
    strips = [jnp.zeros((24, NC), F32) for _ in range(4)]
    for d in range(NH):
        east_turn = turn(acc[2, d], 1)
        west_turn = turn(acc[0, d], -1)
        over_east = jnp.where(lane == 0, east_turn, 0.0)
        over_west = jnp.where(lane == NC - 1, west_turn, 0.0)
        main = acc[1, d] + (east_turn - over_east) + (west_turn - over_west)
        w_main[d] = main
        own = turn(jnp.where(lane < 4, main, 0.0) + over_west, 28)
        own = own + turn(jnp.where(lane >= 124, main, 0.0) + over_east, 4)
        strips[d // 4] = strips[d // 4] + turn(own, 32 * (d % 4))
        k = 16 * (d % 8)
        pack_right[d // 8] = pack_right[d // 8] + turn(jnp.where(lane >= 118, main, 0.0) + over_east, 12 + k)
        pack_left[d // 8] = pack_left[d // 8] + turn(jnp.where(lane < 10, main, 0.0) + over_west, 4 + k)
    for j in range(4):
        w_strip[j] = strips[j]
    for j in range(2):
        to_right[128 + 24 * j:152 + 24 * j, :] = pack_right[j]
        to_left[128 + 24 * j:152 + 24 * j, :] = pack_left[j]

    lane = lanes((8, NC))
    place = lane % 32
    segment = lane // 32
    for r in range(NR):
        right = jnp.zeros((8, NC), F32)
        left = jnp.zeros((8, NC), F32)
        strip_i = jnp.zeros((8, NC), F32)
        strip_s = jnp.zeros((8, NC), F32)
        for g in range(4):
            here = segment == g
            ini = initial[pl.ds(g * 128 + r, 8, stride=NR), :]
            src = source[pl.ds(g * 128 + r, 8, stride=NR), :]
            ini_x[r, 8 * g:8 * g + 8, :] = ini
            src_x[r, 8 * g:8 * g + 8, :] = src
            turned = turn(ini, 4 + 32 * g)
            strip_i = jnp.where(here & (place < 4), turned, strip_i)
            left = jnp.where(here & (place >= 4) & (place < 14), turned, left)
            turned = turn(src, 4 + 32 * g)
            strip_s = jnp.where(here & (place < 4), turned, strip_s)
            left = jnp.where(here & (place >= 20) & (place < 30), turn(src, 20 + 32 * g), left)
            turned = turn(ini, 28 + 32 * g)
            strip_i = jnp.where(here & (place >= 28), turned, strip_i)
            turned = turn(src, 28 + 32 * g)
            strip_s = jnp.where(here & (place >= 28), turned, strip_s)
            right = jnp.where(here & (place >= 18) & (place < 28), turned, right)
            right = jnp.where(here & (place >= 2) & (place < 12), turn(ini, 12 + 32 * g), right)
        ini_x[r, 32:40, :] = strip_i
        src_x[r, 32:40, :] = strip_s
        to_right[8 * r:8 * r + 8, :] = right
        to_left[8 * r:8 * r + 8, :] = left


ROW_I = 0
ROW_S = 10 * 40
ROW_W = ROW_S + 8 * 40
ROW_H = ROW_W + NH * 16
ROW_END = ROW_H + 4 * 16


def columns_body(ini_x, src_x, w_main, w_strip, from_left, from_right,
                 ini_o, src_o, main_o, strip_o, to_up, to_down):
    lane = lanes((8, NC))
    place = lane % 32
    is_left = (place >= 18) & (place < 28)
    is_right = (place >= 4) & (place < 14)
    for r in range(NR):
        left = from_left[8 * r:8 * r + 8, :]
        right = from_right[8 * r:8 * r + 8, :]
        ini_o[r, 0:32, :] = ini_x[r, 0:32, :]
        src_o[r, 0:32, :] = src_x[r, 0:32, :]
        ini_o[r, 32:40, :] = jnp.where(is_left, turn(left, 16), jnp.where(is_right, right, ini_x[r, 32:40, :]))
        src_o[r, 32:40, :] = jnp.where(is_left, left, jnp.where(is_right, turn(right, -16), src_x[r, 32:40, :]))
    lane = lanes((24, NC))
    strips = [w_strip[j] for j in range(4)]
    for d in range(NH):
        k = 16 * (d % 8)
        left = from_left[128 + 24 * (d // 8):152 + 24 * (d // 8), :]
        right = from_right[128 + 24 * (d // 8):152 + 24 * (d // 8), :]
        left = jnp.where((lane >= 18) & (lane <= 28), turn(left, 16 - k), 0.0)
        right = jnp.where((lane >= 3) & (lane <= 13), turn(right, -k), 0.0)
        strips[d // 4] = strips[d // 4] + turn(left + right, 32 * (d % 4))
        main = w_main[d]
        main = main + jnp.where(lane == 0, turn(left, -28), 0.0)
        main = main + jnp.where(lane == NC - 1, turn(right, 124), 0.0)
        main_o[d] = main
        to_up[ROW_W + 16 * d:ROW_W + 16 * d + 16, :] = main[0:16]
        to_down[ROW_W + 16 * d:ROW_W + 16 * d + 16, :] = main[8:24]
    for j in range(4):
        strip_o[j] = strips[j]
        to_up[ROW_H + 16 * j:ROW_H + 16 * j + 16, :] = strips[j][0:16]
        to_down[ROW_H + 16 * j:ROW_H + 16 * j + 16, :] = strips[j][8:24]
    for i in range(10):
        to_up[ROW_I + 40 * i:ROW_I + 40 * i + 40, :] = ini_o[i]
        to_down[ROW_I + 40 * i:ROW_I + 40 * i + 40, :] = ini_o[6 + i]
    for i in range(8):
        to_up[ROW_S + 40 * i:ROW_S + 40 * i + 40, :] = src_o[i]
        to_down[ROW_S + 40 * i:ROW_S + 40 * i + 40, :] = src_o[8 + i]


def basis_body(scale, ini_x, src_x, w_main, w_strip, from_up, from_down, basis, packed,
               coef_m, coef_h, field, sums):
    lane = lanes((8, NC))
    segment = lane // 32
    own = (1, 2, 3)
    for d in range(NH):
        for t in range(5):
            main = None
            strip = None
            parts = []
            if t < 2:
                parts.append((from_up[ROW_W + 16 * d + 8 * t:ROW_W + 16 * d + 8 * t + 8, :],
                              from_up[ROW_H + 16 * (d // 4) + 8 * t:ROW_H + 16 * (d // 4) + 8 * t + 8, :]))
            if t in own:
                parts.append((w_main[d, 8 * t - 8:8 * t, :], w_strip[d // 4, 8 * t - 8:8 * t, :]))
            if t > 2:
                s = 8 * (t - 3)
                parts.append((from_down[ROW_W + 16 * d + s:ROW_W + 16 * d + s + 8, :],
                              from_down[ROW_H + 16 * (d // 4) + s:ROW_H + 16 * (d // 4) + s + 8, :]))
            main = sum(p[0] for p in parts[1:]) + parts[0][0] if len(parts) > 1 else parts[0][0]
            strip = sum(p[1] for p in parts[1:]) + parts[0][1] if len(parts) > 1 else parts[0][1]
            strip = jnp.where(segment == d % 4, strip, 0.0)
            strip = strip + turn(strip, 32)
            strip = strip + turn(strip, 64)
            coef_m[d, 8 * t:8 * t + 8, :] = main
            coef_h[d, 8 * t:8 * t + 8, :] = strip
            dc = HALF[d][1]
            if dc != 0:
                turned = turn(main, dc)
                if dc > 0:
                    turned = jnp.where(lane < dc, turn(strip, dc - 28), turned)
                else:
                    turned = jnp.where(lane >= NC + dc, turn(strip, dc + 124), turned)
                i = TURNED_INDEX[HALF[d]]
                coef_m[i, 8 * t:8 * t + 8, :] = turned
                coef_h[i, 8 * t:8 * t + 8, :] = turn(strip, dc)

    for i in range(10):
        field[0, i] = from_up[ROW_I + 40 * i:ROW_I + 40 * i + 40, :]
        field[0, 26 + i] = from_down[ROW_I + 40 * i:ROW_I + 40 * i + 40, :]
    for i in range(8):
        field[1, 2 + i] = from_up[ROW_S + 40 * i:ROW_S + 40 * i + 40, :]
        field[1, 26 + i] = from_down[ROW_S + 40 * i:ROW_S + 40 * i + 40, :]
    for i in range(NR):
        field[0, 10 + i] = ini_x[i]
        field[1, 10 + i] = src_x[i]

    place = lane % 32

    def image(buffer, r):
        def unit(coef, u):
            near = [field[buffer, r + 10 + dr, 8 * u:8 * u + 8, :] for dr in range(-2, 3)]
            out = None
            for dc in (0, 1, -1, 2, -2):
                part = None
                for dr in range(-2, 3):
                    term = coef[(dr, dc)] * near[dr + 2]
                    part = term if part is None else part + term
                out = part if out is None else out + turn(part, -dc)
            return out

        def spread(ref):
            coef = {}
            for dr in range(-2, 3):
                for dc in range(-2, 3):
                    if (dr, dc) in HALF_INDEX:
                        index = TURNED_INDEX[(dr, dc)] if dc != 0 else HALF_INDEX[(dr, dc)]
                        at = r + 15
                    else:
                        index = HALF_INDEX[(-dr, -dc)]
                        at = r + 15 + dr
                    coef[(dr, dc)] = jnp.broadcast_to(ref[index, pl.ds(at, 1), :], (8, NC))
            return coef

        coef = spread(coef_m)
        mains = [unit(coef, g) for g in range(4)]
        strip = unit(spread(coef_h), 4)
        fixed = strip
        result = []
        for g in range(4):
            here = segment == g
            fixed = jnp.where(here & (place >= 30), turn(mains[g], 32 * g + 28), fixed)
            fixed = jnp.where(here & (place < 2), turn(mains[g], 32 * g + 4), fixed)
            out = jnp.where(lane < 2, turn(strip, 100 - 32 * g), mains[g])
            result.append(jnp.where(lane >= 126, turn(strip, 124 - 32 * g), out))
        return result + [fixed]

    def start_row(i, carry):
        r = i - 8
        units = image(0, r)
        for u in range(5):
            field[2, r + 10, 8 * u:8 * u + 8, :] = field[1, r + 10, 8 * u:8 * u + 8, :] - units[u]
        return carry

    lax.fori_loop(0, 32, start_row, 0)
    for r in range(NR):
        basis[r, 0:32, :] = field[2, r + 10, 0:32, :]
    for step in range(STEPS):
        reach = 6 - 2 * step
        old, new = 2 + step % 2, 3 - step % 2

        def step_row(i, carry, step=step, reach=reach, old=old, new=new):
            r = i - reach
            units = image(old, r)
            if step + 1 < STEPS:
                for u in range(5):
                    field[new, r + 10, 8 * u:8 * u + 8, :] = units[u] - 2.0 * field[old, r + 10, 8 * u:8 * u + 8, :]

            def keep():
                for u in range(4):
                    basis[r, 32 + 32 * step + 8 * u:40 + 32 * step + 8 * u, :] = units[u]

            if reach == 0:
                keep()
            else:
                pl.when((r >= 0) & (r < NR))(keep)
            return carry

        lax.fori_loop(0, NR + 2 * reach, step_row, 0)

    sums[...] = jnp.zeros(sums.shape, F32)

    def product(i, carry):
        pair = jnp.concatenate([basis[2 * i], basis[2 * i + 1]], axis=1)
        sums[...] += lax.dot_general(pair, pair[32:], (((1,), (1,)), ((), ())),
                                     precision=lax.Precision.HIGHEST, preferred_element_type=F32)
        return carry

    lax.fori_loop(0, NR // 2, product, 0)
    lane = lanes((32, NC))
    odd = jnp.zeros((32, NC), F32)
    even = jnp.zeros((32, NC), F32)
    for b in range(4):
        odd = jnp.where(lane // 32 == b, sums[32 * b:32 * b + 32, :], odd)
        even = jnp.where(lane // 32 == b, sums[32 + 32 * b:64 + 32 * b, :], even)
    odd = odd * scale
    even = even * scale
    row = lax.broadcasted_iota(jnp.int32, (32, NC), 0)
    within = lane % 32
    packed[0:32, :] = jnp.where(within >= row, odd, even)
    diagonal = jnp.sum(jnp.where(within == row, even, 0.0), axis=0, keepdims=True)
    packed[32:40, :] = jnp.broadcast_to(diagonal, (8, NC))


def solve_body(parts, basis, out, upper):
    total = parts[0]
    for i in range(1, parts.shape[0]):
        total = total + parts[i]
    half = total[0:32]
    lane = lanes((32, NC))
    row = lax.broadcasted_iota(jnp.int32, (32, NC), 0)
    within = lane % 32
    block = lane // 32
    flipped = jnp.transpose(jnp.concatenate([half] * 4, axis=0))
    mirror = flipped[0:32]
    for b in range(1, 4):
        mirror = jnp.where(block == b, flipped[32 * b:32 * b + 32], mirror)
    odd = jnp.where(within >= row, half, mirror)
    even = jnp.where(within < row, half, jnp.where(within > row, mirror, jnp.broadcast_to(total[32:33], (32, NC))))

    def pick(a, b, c, d):
        return jnp.where(block == 0, a, jnp.where(block == 1, b, jnp.where(block == 2, c, d)))

    odd_up, odd_down, even_up, even_down = turn(odd, 32), turn(odd, -32), turn(even, 32), turn(even, -32)
    gram = [
        pick(even, odd, even_up, odd_up),
        pick(odd_down, even, odd, even_up),
        pick(even_down, odd_down, even, odd),
        pick(turn(odd, -64), even_down, odd_down, even),
    ]
    first = jnp.where(lane < 32, odd, 0.0)
    second = jnp.where(lane < 32, even, 0.0) - 2.0 * first
    third = jnp.where(lane < 32, odd_down, 0.0) - 2.0 * second
    fourth = jnp.where(lane < 32, even_down, 0.0) - 2.0 * third
    right = [first, second, third, fourth]
    g = [gram[t // 4][8 * (t % 4):8 * (t % 4) + 8] for t in range(16)]
    p = [right[t // 4][8 * (t % 4):8 * (t % 4) + 8] for t in range(16)]
    lane = lanes((8, NC))
    sub = lax.broadcasted_iota(jnp.int32, (8, NC), 0)
    for k in range(128):
        t, j = divmod(k, 8)
        u = jnp.broadcast_to(g[t][j:j + 1, :], (8, NC))
        up = jnp.broadcast_to(p[t][j:j + 1, :], (8, NC))
        d = jnp.broadcast_to(u[:, k:k + 1], (8, NC))
        inverse = 1.0 / d
        line = jnp.where(lane >= k, u / jnp.sqrt(d), 0.0)
        upper[k:k + 1, :] = line[0:1]
        for i in range(16):
            m = jnp.broadcast_to(g[i][:, k:k + 1], (8, NC)) * inverse
            if i == t:
                g[i] = jnp.where(sub == j, g[i] * inverse, g[i] - m * u)
                p[i] = jnp.where(sub == j, p[i] * inverse, p[i] - m * up)
            else:
                g[i] = g[i] - m * u
                p[i] = p[i] - m * up
    weights = jnp.transpose(jnp.concatenate(p, axis=0))[0:32]
    for r in range(NR):
        moved = jnp.dot(weights, basis[r, 32:160, :], precision=lax.Precision.HIGHEST, preferred_element_type=F32)
        out[pl.ds(r, 32, stride=NR), :] = basis[r, 0:32, :] - moved


def shape(*dims):
    return jax.ShapeDtypeStruct(dims, F32)


def neighbours(count, step):
    return [(i, i + step) for i in range(count) if 0 <= i + step < count]


def on_device(dom, sub, dom_count, sub_count, reduce_groups, source, initial, lumped_mass, node_slots, stiffness):
    rows_total, cols_total = dom_count * NR, sub_count * NC
    pos = jnp.stack([lax.axis_index(dom), lax.axis_index(sub)]).astype(jnp.int32)

    def prepare(*refs):
        prepare_body(rows_total, cols_total, *refs)

    ini_x, src_x, w_main, w_strip, to_left, to_right = call(
        prepare,
        (shape(NR, 40, NC), shape(NR, 40, NC), shape(NH, 24, NC), shape(4, 24, NC), shape(176, NC), shape(176, NC)),
        scratch=[pltpu.VMEM((3, NH, 24, NC), F32)],
        in_specs=[pl.BlockSpec(memory_space=pltpu.SMEM)] + vmem_specs(5),
        out_specs=tuple(vmem_specs(6)),
        name="prepare",
    )(pos, source.reshape(NF * NR, NC), initial.reshape(NF * NR, NC), lumped_mass, node_slots,
      stiffness.reshape(36, NR, NC))
    from_right = lax.ppermute(to_left, sub, neighbours(sub_count, -1))
    from_left = lax.ppermute(to_right, sub, neighbours(sub_count, 1))
    ini_x, src_x, w_main, w_strip, to_up, to_down = call(
        columns_body,
        (shape(NR, 40, NC), shape(NR, 40, NC), shape(NH, 24, NC), shape(4, 24, NC), shape(ROW_END, NC),
         shape(ROW_END, NC)),
        name="columns",
    )(ini_x, src_x, w_main, w_strip, from_left, from_right)
    from_down = lax.ppermute(to_up, dom, neighbours(dom_count, -1))
    from_up = lax.ppermute(to_down, dom, neighbours(dom_count, 1))

    def products(*refs):
        basis_body(1.0 / float(rows_total * cols_total), *refs)

    basis, packed = call(
        products,
        (shape(NR, 160, NC), shape(40, NC)),
        scratch=[
            pltpu.VMEM((NCOEF, 40, NC), F32),
            pltpu.VMEM((NCOEF, 40, NC), F32),
            pltpu.VMEM((4, 36, 40, NC), F32),
            pltpu.VMEM((160, NC), F32),
        ],
        name="products",
    )(ini_x, src_x, w_main, w_strip, from_up, from_down)
    for i, (axes, count) in enumerate(reduce_groups):
        if count == 2:
            gathered = jnp.stack([packed, lax.ppermute(packed, axes, [(0, 1), (1, 0)])])
        else:
            gathered = lax.all_to_all(jnp.broadcast_to(packed[None], (count, 40, NC)), axes, 0, 0)
        if i + 1 < len(reduce_groups):
            packed = jnp.sum(gathered, axis=0)
    new_residual, upper = call(
        solve_body,
        (shape(NF * NR, NC), shape(128, 128)),
        name="solve",
    )(gathered, basis)
    return (new_residual.reshape(NF, NR, NC), upper)


def solution(mesh):
    dom_count, sub_count = mesh.shape["dom"], mesh.shape["sub"]
    if dom_count == 64 and sub_count == 4:
        fine = Mesh(mesh.devices.reshape(8, 4, 2, 4), ("z", "x", "c", "sub"))
        dom = ("z", "x", "c")
        groups = ((("c",), 2), (("x", "sub"), 16), (("z",), 8))
    else:
        fine, dom = mesh, ("dom",)
        groups = (("sub", sub_count), ("dom", dom_count))

    def body(*args):
        return on_device(dom, "sub", dom_count, sub_count, groups, *args)

    return jax.shard_map(
        body,
        mesh=fine,
        in_specs=(
            P(None, dom, "sub"),
            P(None, dom, "sub"),
            P(dom, "sub"),
            P(None, dom, "sub"),
            P(None, None, dom, "sub"),
        ),
        out_specs=(P(None, dom, "sub"), P()),
        check_vma=False,
    )
```

time: 668 us -> 119 us (0.18); the launches traced: 656 us -> 119 us
  waiting for transfers between devices: 248 us -> 14.2 us
  local copies, waits for them, and re-layouts: 119 us -> 1.48 us
  starting transfers between devices: 96.8 us -> 12.3 us
  other arithmetic: 74 us -> 1.38 us
  blocking collectives: 97.4 us -> 32.9 us
  Pallas kernels: 0 us -> 55.5 us
  between operations: 17.4 us -> 0.69 us
    psum x1 -> x0, waiting for transfers between devices: 161 us -> none  [on_device(): gram, projected = lax.psum((gram_local, projected_local), ('dom', 'sub'))]
    scatter-add x45 -> x0, local copies, waits for them, and re-layouts: 106 us -> none  [the longest x35 98.1 us: apply(): accum = accum.at[:, 1 + row_p:1 + row_p + height, 1 + col_p:1 + col_p + b...]
    psum x1 -> x0, blocking collectives: 97.4 us -> none  [on_device(): gram, projected = lax.psum((gram_local, projected_local), ('dom', 'sub'))]
    ppermute x40 -> x5, starting transfers between devices: 96.7 us -> 12.3 us  [the longest x1 5.1 us: on_device(): from_up = lax.ppermute(to_down, dom, neighbours(dom_count, 1))]
    ppermute x40 -> x5, waiting for transfers between devices: 87 us -> 14.2 us  [the longest x1 4.32 us: on_device(): from_up = lax.ppermute(to_down, dom, neighbours(dom_count, 1))]
    pallas_call x0 -> x4, Pallas kernels: none -> 55.5 us  [the longest x1 27.9 us: on_device(): call(products, (shape(NR, 160, NC), shape(40, NC)), scratch=[pltpu.VMEM((...]
    another operation x11 -> x1, other arithmetic: 38.2 us -> 0.62 us  [on_device(): jnp.stack([lax.axis_index(dom), lax.axis_index(sub)]).astype(jnp.int32)]
    all_to_all x0 -> x2, blocking collectives: none -> 32.9 us  [on_device(): lax.all_to_all(jnp.broadcast_to(packed[None], (count, 40, NC)), axes, 0, 0)]
  transfers between devices with their start and end apart: 41 -> 5, of which waited for: 30 -> 5; matrix products, arithmetic and copies ran while one was open for 1% -> 0% of each run, Pallas kernels for 0% -> 0%
where the time goes in v1:
time: 119 us
  Pallas kernels  55.5 us (47%)
  blocking collectives  32.9 us (28%)
  waiting for transfers between devices  14.2 us (12%)
  starting transfers between devices  12.3 us (10%)
  local copies, waits for them, and re-layouts  1.48 us (1%)
  other arithmetic  1.38 us (1%)
    all_to_all x2, blocking collectives, on_device(): lax.all_to_all(jnp.broadcast_to(packed[None], (count, 40, NC)), axes, 0, 0)  32.9 us
    pallas_call x1, Pallas kernels, on_device(): call(products, (shape(NR, 160, NC), shape(40, NC)), scratch=[pltpu.VMEM((...  27.9 us
    pallas_call x1, Pallas kernels, on_device(): call(solve_body, (shape(NF * NR, NC), shape(128, 128)), name='solve')  20.7 us
    ppermute x1, starting transfers between devices, on_device(): from_up = lax.ppermute(to_down, dom, neighbours(dom_count, 1))  5.1 us
    ppermute x1, waiting for transfers between devices, on_device(): from_up = lax.ppermute(to_down, dom, neighbours(dom_count, 1))  4.32 us
    ppermute x1, waiting for transfers between devices, on_device(): from_down = lax.ppermute(to_up, dom, neighbours(dom_count, -1))  4.29 us
    ppermute x1, starting transfers between devices, on_device(): from_left = lax.ppermute(to_right, sub, neighbours(sub_count, 1))  4.01 us
    pallas_call x1, Pallas kernels, on_device(): call(prepare, (shape(NR, 40, NC), shape(NR, 40, NC), shape(NH, 24, NC), s...  3.8 us
  transfers between devices with their start and end apart: 5, of which 5 were waited for; matrix products, arithmetic and copies ran while one was open for 0% of the time, Pallas kernels for 0%

profile of v1, /device:TPU:1, one launch (start us, length us, event | category | flops | bytes accessed | tf_op | source)
XLA Modules:
  0.0 118.5 jit_solution(16467477551528184476)
XLA Ops:
  0.6 0.6 pad_add_fusion.refs_0_
  1.3 3.8 %prepare.1 = (f32[16,40,128]{2,1,0:T(8,128)}, f32[16,40,128]{2,1,0:T(8,128)}, f32[13,24,128]{2,1,0:T(8,128)}, f32[4,24,128]{2,1,0:T(8,128)}, f32[176,128]{1,0:T(8,128)}, /*index=5*/f32[176,128]{1,0:T(8,128)}) custom-call(s32[2]{0:T(128)} %pad_add_fusion.refs_0_, f32[512,128]{1,0:T(8,128)} %bitcast.7, f32[512,128]{1,0:T(8,128)} %bitcast.8, ...), custom_call_target="tpu_custom_call" | custom-call | tf_op jit(solution)/shard_map/prepare/pallas_call | solution.py:397
  5.1 4.0 %collective-permute-start = (f32[176,128]{1,0:T(8,128)}, f32[176,128]{1,0:T(8,128)S(1)}, u32[]{:S(2)}, u32[]{:S(2)}) collective-permute-start(f32[176,128]{1,0:T(8,128)} %get-tuple-element.22), channel_id=1, source_target_pairs={{0,1},{1,2},{2,3},{4,5},{5,6},{6,7},{8,9},{9,10},{10,11},{12,13},{... | collective-permute-start | bytes 270344 | tf_op jit(solution)/shard_map/ppermute | solution.py:407
  9.1 1.3 %collective-permute-start.1 = (f32[176,128]{1,0:T(8,128)}, f32[176,128]{1,0:T(8,128)S(1)}, u32[]{:S(2)}, u32[]{:S(2)}) collective-permute-start(f32[176,128]{1,0:T(8,128)} %get-tuple-element.23), channel_id=1, source_target_pairs={{1,0},{2,1},{3,2},{5,4},{6,5},{7,6},{9,8},{10,9},{11,10},{13,12},{... | collective-permute-start | bytes 270344 | tf_op jit(solution)/shard_map/ppermute | solution.py:406
  10.4 0.6 collective-permute-done.from_left
  10.9 0.0 copy-start.2
  10.9 3.6 %collective-permute-done.1.from_right = f32[176,128]{1,0:T(8,128)S(1)} collective-permute-done((f32[176,128]{1,0:T(8,128)}, f32[176,128]{1,0:T(8,128)S(1)}, u32[]{:S(2)}, u32[]{:S(2)}) %collective-permute-start.1) | collective-permute-done | bytes 90144 | tf_op jit(solution)/shard_map/ppermute | solution.py:406
  14.6 0.0 copy-start.3
  14.6 0.0 copy-done.2
  14.6 0.6 copy-done.3
  15.2 3.1 %columns.1 = (f32[16,40,128]{2,1,0:T(8,128)}, f32[16,40,128]{2,1,0:T(8,128)}, f32[13,24,128]{2,1,0:T(8,128)}, f32[4,24,128]{2,1,0:T(8,128)}, f32[992,128]{1,0:T(8,128)}, /*index=5*/f32[992,128]{1,0:T(8,128)}) custom-call(f32[16,40,128]{2,1,0:T(8,128)} %get-tuple-element.18.ini_x, f32[16,40,128]{2,1,0:T(8,128)} %get-tuple-element.19.src_x, ...), custom_call_target="tpu_custom_call" | custom-call | tf_op jit(solution)/shard_map/columns/pallas_call | solution.py:408
  18.3 5.1 %collective-permute-start.2 = (f32[992,128]{1,0:T(8,128)}, f32[992,128]{1,0:T(8,128)S(1)}, u32[]{:S(2)}, u32[]{:S(2)}) collective-permute-start(f32[992,128]{1,0:T(8,128)} %get-tuple-element.28), channel_id=1, source_target_pairs={{0,4},{4,8},{8,12},{12,16},{16,20},{20,24},{24,28},{28,32},{32,36}... | collective-permute-start | bytes 1523720 | tf_op jit(solution)/shard_map/ppermute | solution.py:415
  23.4 1.9 %collective-permute-start.3 = (f32[992,128]{1,0:T(8,128)}, f32[992,128]{1,0:T(8,128)S(1)}, u32[]{:S(2)}, u32[]{:S(2)}) collective-permute-start(f32[992,128]{1,0:T(8,128)} %get-tuple-element.29), channel_id=1, source_target_pairs={{4,0},{8,4},{12,8},{16,12},{20,16},{24,20},{28,24},{32,28},{36,32}... | collective-permute-start | bytes 1523720 | tf_op jit(solution)/shard_map/ppermute | solution.py:414
  25.3 4.3 %collective-permute-done.2.refs_4_ = f32[992,128]{1,0:T(8,128)S(1)} collective-permute-done((f32[992,128]{1,0:T(8,128)}, f32[992,128]{1,0:T(8,128)S(1)}, u32[]{:S(2)}, u32[]{:S(2)}) %collective-permute-start.2) | collective-permute-done | bytes 507936 | tf_op jit(solution)/shard_map/ppermute | solution.py:415
  29.7 0.0 copy-start
  29.7 4.3 %collective-permute-done.3.refs_5_ = f32[992,128]{1,0:T(8,128)S(1)} collective-permute-done((f32[992,128]{1,0:T(8,128)}, f32[992,128]{1,0:T(8,128)S(1)}, u32[]{:S(2)}, u32[]{:S(2)}) %collective-permute-start.3) | collective-permute-done | bytes 507936 | tf_op jit(solution)/shard_map/ppermute | solution.py:414
  34.0 0.0 copy-start.1
  34.0 0.0 copy-done
  34.0 0.8 copy-done.1
  34.8 27.9 %products.1 = (f32[16,160,128]{2,1,0:T(8,128)}, f32[40,128]{1,0:T(8,128)}) custom-call(f32[16,40,128]{2,1,0:T(8,128)} %get-tuple-element.24.refs_0_, f32[16,40,128]{2,1,0:T(8,128)} %get-tuple-element.25.refs_1_, f32[13,24,128]{2,1,0:T(8,128)} %get-tuple-element.26.refs_2_, f32[4,24,128]{2,1,0:T(8,128)} %get-tuple-element.27.refs_3_, f32[992,128]{1,0:T(8,128)} %copy-done, ...), custom_call_target="tpu_custom_call" | custom-call | tf_op jit(solution)/shard_map/products/pallas_call | solution.py:420
  62.7 0.0 collective-permute-start.4
  62.7 1.4 %collective-permute-done.4 = f32[40,128]{1,0:T(8,128)S(1)} collective-permute-done((f32[40,128]{1,0:T(8,128)}, f32[40,128]{1,0:T(8,128)S(1)}, u32[]{:S(2)}, u32[]{:S(2)}) %collective-permute-start.4) | collective-permute-done | bytes 20512 | tf_op jit(solution)/shard_map/ppermute | solution.py:433
  64.1 0.7 reduce_sum.17
  64.8 16.6 %all_to_all.10 = f32[16,40,128]{2,1,0:T(8,128)S(1)} all-to-all(f32[16,40,128]{2,1,0:T(8,128)S(1)} %broadcast_in_dim.4), channel_id=1, replica_groups=mesh['z'=8,'x'=4,'c'=2,'sub'=4] {'x','sub'}, dimensions={0} | all-to-all | bytes 655360 | tf_op jit(solution)/shard_map/all_to_all | solution.py:435
  81.5 16.3 %all_to_all.11.parts = f32[8,40,128]{2,1,0:T(8,128)} all-to-all(f32[8,40,128]{2,1,0:T(8,128)S(1)} %broadcast_in_dim.5), channel_id=1, replica_groups=mesh['z'=8,'x'=4,'c'=2,'sub'=4] {'z'}, dimensions={0} | all-to-all | bytes 327680 | tf_op jit(solution)/shard_map/all_to_all | solution.py:435
  97.8 20.7 %solve.1 = (f32[512,128]{1,0:T(8,128)}, f32[128,128]{1,0:T(8,128)}) custom-call(f32[8,40,128]{2,1,0:T(8,128)} %all_to_all.11.parts, f32[16,160,128]{2,1,0:T(8,128)} %get-tuple-element.31.basis), custom_call_target="tpu_custom_call" | custom-call | tf_op jit(solution)/shard_map/solve/pallas_call | solution.py:438
  (3 shorter events, 0.1 us)
Async XLA Ops:
  5.1 5.9 %collective-permute-start = (f32[176,128]{1,0:T(8,128)}, f32[176,128]{1,0:T(8,128)S(1)}, u32[]{:S(2)}, u32[]{:S(2)}) collective-permute-start(f32[176,128]{1,0:T(8,128)} %get-tuple-element.22), channel_id=1, source_target_pairs={{0,1},{1,2},{2,3},{4,5},{5,6},{6,7},{8,9},{9,10},{10,11},{12,13},{... | collective-permute-start | bytes 270344 | tf_op jit(solution)/shard_map/ppermute | solution.py:407
  9.1 5.5 %collective-permute-start.1 = (f32[176,128]{1,0:T(8,128)}, f32[176,128]{1,0:T(8,128)S(1)}, u32[]{:S(2)}, u32[]{:S(2)}) collective-permute-start(f32[176,128]{1,0:T(8,128)} %get-tuple-element.23), channel_id=1, source_target_pairs={{1,0},{2,1},{3,2},{5,4},{6,5},{7,6},{9,8},{10,9},{11,10},{13,12},{... | collective-permute-start | bytes 270344 | tf_op jit(solution)/shard_map/ppermute | solution.py:406
  10.9 3.6 %copy-start.2 = (f32[176,128]{1,0:T(8,128)}, f32[176,128]{1,0:T(8,128)S(1)}, u32[]{:S(2)}) copy-start(f32[176,128]{1,0:T(8,128)S(1)} %collective-permute-done.from_left) | copy-start | bytes 270340
  14.6 0.6 copy-start.3
  18.3 11.3 %collective-permute-start.2 = (f32[992,128]{1,0:T(8,128)}, f32[992,128]{1,0:T(8,128)S(1)}, u32[]{:S(2)}, u32[]{:S(2)}) collective-permute-start(f32[992,128]{1,0:T(8,128)} %get-tuple-element.28), channel_id=1, source_target_pairs={{0,4},{4,8},{8,12},{12,16},{16,20},{20,24},{24,28},{28,32},{32,36}... | collective-permute-start | bytes 1523720 | tf_op jit(solution)/shard_map/ppermute | solution.py:415
  23.4 10.5 %collective-permute-start.3 = (f32[992,128]{1,0:T(8,128)}, f32[992,128]{1,0:T(8,128)S(1)}, u32[]{:S(2)}, u32[]{:S(2)}) collective-permute-start(f32[992,128]{1,0:T(8,128)} %get-tuple-element.29), channel_id=1, source_target_pairs={{4,0},{8,4},{12,8},{16,12},{20,16},{24,20},{28,24},{32,28},{36,32}... | collective-permute-start | bytes 1523720 | tf_op jit(solution)/shard_map/ppermute | solution.py:414
  29.7 4.3 %copy-start = (f32[992,128]{1,0:T(8,128)}, f32[992,128]{1,0:T(8,128)S(1)}, u32[]{:S(2)}) copy-start(f32[992,128]{1,0:T(8,128)S(1)} %collective-permute-done.2.refs_4_) | copy-start | bytes 1523716
  34.0 0.8 copy-start.1
  62.7 1.4 %collective-permute-start.4 = (f32[40,128]{1,0:T(8,128)}, f32[40,128]{1,0:T(8,128)S(1)}, u32[]{:S(2)}, u32[]{:S(2)}) collective-permute-start(f32[40,128]{1,0:T(8,128)} %get-tuple-element.30), channel_id=1, source_target_pairs={{0,4},{4,0},{1,5},{5,1},{2,6},{6,2},{3,7},{7,3},{8,12},{12,8},{9,1... | collective-permute-start | bytes 61448 | tf_op jit(solution)/shard_map/ppermute | solution.py:433

commit v2 on v1

--- a/solution.py
+++ b/solution.py
@@ -179,7 +179,7 @@
 
 
 def basis_body(scale, ini_x, src_x, w_main, w_strip, from_up, from_down, basis, packed,
-               coef_m, coef_h, field, sums):
+               coef_m, coef_h, ini_v, src_v, vec_a, vec_b, sums):
     lane = lanes((8, NC))
     segment = lane // 32
     own = (1, 2, 3)
@@ -216,29 +216,22 @@
                 coef_h[i, 8 * t:8 * t + 8, :] = turn(strip, dc)
 
     for i in range(10):
-        field[0, i] = from_up[ROW_I + 40 * i:ROW_I + 40 * i + 40, :]
-        field[0, 26 + i] = from_down[ROW_I + 40 * i:ROW_I + 40 * i + 40, :]
+        ini_v[i] = from_up[ROW_I + 40 * i:ROW_I + 40 * i + 40, :]
+        ini_v[26 + i] = from_down[ROW_I + 40 * i:ROW_I + 40 * i + 40, :]
     for i in range(8):
-        field[1, 2 + i] = from_up[ROW_S + 40 * i:ROW_S + 40 * i + 40, :]
-        field[1, 26 + i] = from_down[ROW_S + 40 * i:ROW_S + 40 * i + 40, :]
+        src_v[2 + i] = from_up[ROW_S + 40 * i:ROW_S + 40 * i + 40, :]
+        src_v[26 + i] = from_down[ROW_S + 40 * i:ROW_S + 40 * i + 40, :]
     for i in range(NR):
-        field[0, 10 + i] = ini_x[i]
-        field[1, 10 + i] = src_x[i]
+        ini_v[10 + i] = ini_x[i]
+        src_v[10 + i] = src_x[i]
 
     place = lane % 32
-
-    def image(buffer, r):
-        def unit(coef, u):
-            near = [field[buffer, r + 10 + dr, 8 * u:8 * u + 8, :] for dr in range(-2, 3)]
-            out = None
-            for dc in (0, 1, -1, 2, -2):
-                part = None
-                for dr in range(-2, 3):
-                    term = coef[(dr, dc)] * near[dr + 2]
-                    part = term if part is None else part + term
-                out = part if out is None else out + turn(part, -dc)
-            return out
-
+    inner = jnp.where((place >= 30) | (place < 2), segment, 4)
+    tail = place >= 30
+    head = lane < 2
+    foot = lane >= NC - 2
+
+    def image(vec, r):
         def spread(ref):
             coef = {}
             for dr in range(-2, 3):
@@ -252,77 +245,119 @@
                     coef[(dr, dc)] = jnp.broadcast_to(ref[index, pl.ds(at, 1), :], (8, NC))
             return coef
 
+        def unit(coef, u):
+            near = [vec[r + 10 + dr, 8 * u:8 * u + 8, :] for dr in range(-2, 3)]
+            parts = []
+            for dc in (-2, 2, -1, 1, 0):
+                part = None
+                for dr in range(-2, 3):
+                    term = coef[(dr, dc)] * near[dr + 2]
+                    part = term if part is None else part + term
+                parts.append(turn(part, -dc))
+            return ((parts[0] + parts[1]) + (parts[2] + parts[3])) + parts[4]
+
+        coef_strip = spread(coef_h)
+        strip = unit(coef_strip, 4)
         coef = spread(coef_m)
-        mains = [unit(coef, g) for g in range(4)]
-        strip = unit(spread(coef_h), 4)
         fixed = strip
         result = []
         for g in range(4):
-            here = segment == g
-            fixed = jnp.where(here & (place >= 30), turn(mains[g], 32 * g + 28), fixed)
-            fixed = jnp.where(here & (place < 2), turn(mains[g], 32 * g + 4), fixed)
-            out = jnp.where(lane < 2, turn(strip, 100 - 32 * g), mains[g])
-            result.append(jnp.where(lane >= 126, turn(strip, 124 - 32 * g), out))
+            main = unit(coef, g)
+            edge = jnp.where(tail, turn(main, 32 * g + 28), turn(main, 32 * g + 4))
+            fixed = jnp.where(inner == g, edge, fixed)
+            out = jnp.where(head, turn(strip, 100 - 32 * g), main)
+            result.append(jnp.where(foot, turn(strip, 124 - 32 * g), out))
         return result + [fixed]
 
-    def start_row(i, carry):
-        r = i - 8
-        units = image(0, r)
-        for u in range(5):
-            field[2, r + 10, 8 * u:8 * u + 8, :] = field[1, r + 10, 8 * u:8 * u + 8, :] - units[u]
+    vectors = (vec_a, vec_b)
+    for step in range(-1, STEPS):
+        reach = 6 - 2 * step
+        source_vec = ini_v if step < 0 else vectors[step % 2]
+        target_vec = vec_a if step < 0 else vectors[(step + 1) % 2]
+
+        def some_rows(rows, inside, step=step, source_vec=source_vec, target_vec=target_vec):
+            values = []
+            for r in rows:
+                units = image(source_vec, r)
+                olds = src_v if step < 0 else source_vec
+                nexts = []
+                if step + 1 < STEPS:
+                    for u in range(5):
+                        old = olds[r + 10, 8 * u:8 * u + 8, :]
+                        nexts.append(old - units[u] if step < 0 else units[u] - 2.0 * old)
+                values.append((r, units, nexts))
+            for r, units, nexts in values:
+                for u, value in enumerate(nexts):
+                    target_vec[r + 10, 8 * u:8 * u + 8, :] = value
+                if inside:
+                    kept = nexts if step < 0 else units
+                    for u in range(4):
+                        at = 32 + 32 * step + 8 * u
+                        basis[r, at:at + 8, :] = kept[u]
+
+        def outer(i, carry, reach=reach, some_rows=some_rows):
+            top = 2 * i - reach
+            bottom = NR + 2 * i
+            some_rows((top, top + 1, bottom, bottom + 1), False)
+            return carry
+
+        def middle(i, carry, some_rows=some_rows):
+            some_rows(tuple(4 * i + j for j in range(4)), True)
+            return carry
+
+        if reach > 0:
+            lax.fori_loop(0, reach // 2, outer, 0)
+        lax.fori_loop(0, NR // 4, middle, 0)
+
+    sums[...] = jnp.zeros(sums.shape, F32)
+
+    def product(i, carry):
+        total = None
+        for j in range(2):
+            r = 4 * i + 2 * j
+            high, mid, low = split(jnp.concatenate([basis[r], basis[r + 1]], axis=1))
+            left = [jnp.concatenate([x[0:32], x[96:160]], axis=0) for x in (high, mid, low)]
+            both = jnp.concatenate([high[32:], mid[32:]], axis=0)
+            hh = matmul_t(left[0], both)
+            mm = matmul_t(left[1], both)
+            rest = matmul_t(left[2], high[32:]) + matmul_t(left[0], low[32:])
+            part = ((rest + mm[:, NC:]) + (hh[:, NC:] + mm[:, :NC])) + hh[:, :NC]
+            total = part if total is None else total + part
+        sums[...] += total
         return carry
 
-    lax.fori_loop(0, 32, start_row, 0)
-    for r in range(NR):
-        basis[r, 0:32, :] = field[2, r + 10, 0:32, :]
-    for step in range(STEPS):
-        reach = 6 - 2 * step
-        old, new = 2 + step % 2, 3 - step % 2
-
-        def step_row(i, carry, step=step, reach=reach, old=old, new=new):
-            r = i - reach
-            units = image(old, r)
-            if step + 1 < STEPS:
-                for u in range(5):
-                    field[new, r + 10, 8 * u:8 * u + 8, :] = units[u] - 2.0 * field[old, r + 10, 8 * u:8 * u + 8, :]
-
-            def keep():
-                for u in range(4):
-                    basis[r, 32 + 32 * step + 8 * u:40 + 32 * step + 8 * u, :] = units[u]
-
-            if reach == 0:
-                keep()
-            else:
-                pl.when((r >= 0) & (r < NR))(keep)
-            return carry
-
-        lax.fori_loop(0, NR + 2 * reach, step_row, 0)
-
-    sums[...] = jnp.zeros(sums.shape, F32)
-
-    def product(i, carry):
-        pair = jnp.concatenate([basis[2 * i], basis[2 * i + 1]], axis=1)
-        sums[...] += lax.dot_general(pair, pair[32:], (((1,), (1,)), ((), ())),
-                                     precision=lax.Precision.HIGHEST, preferred_element_type=F32)
-        return carry
-
-    lax.fori_loop(0, NR // 2, product, 0)
+    lax.fori_loop(0, NR // 4, product, 0)
     lane = lanes((32, NC))
-    odd = jnp.zeros((32, NC), F32)
-    even = jnp.zeros((32, NC), F32)
-    for b in range(4):
-        odd = jnp.where(lane // 32 == b, sums[32 * b:32 * b + 32, :], odd)
-        even = jnp.where(lane // 32 == b, sums[32 + 32 * b:64 + 32 * b, :], even)
-    odd = odd * scale
-    even = even * scale
+    low_half = sums[0:32, :] * scale
+    high_half = jnp.where(lane < 64, turn(sums[32:64, :], -32), sums[64:96, :]) * scale
     row = lax.broadcasted_iota(jnp.int32, (32, NC), 0)
     within = lane % 32
-    packed[0:32, :] = jnp.where(within >= row, odd, even)
-    diagonal = jnp.sum(jnp.where(within == row, even, 0.0), axis=0, keepdims=True)
+    packed[0:32, :] = jnp.where(within >= row, low_half, high_half)
+    diagonal = jnp.sum(jnp.where(within == row, high_half, 0.0), axis=0, keepdims=True)
     packed[32:40, :] = jnp.broadcast_to(diagonal, (8, NC))
 
 
-def solve_body(parts, basis, out, upper):
+def split(value):
+    high = value.astype(jnp.bfloat16)
+    value = value - high.astype(F32)
+    mid = value.astype(jnp.bfloat16)
+    return high, mid, (value - mid.astype(F32)).astype(jnp.bfloat16)
+
+
+def matmul_t(a, b):
+    return lax.dot_general(a, b, (((1,), (1,)), ((), ())), preferred_element_type=F32)
+
+
+def matmul(a, b):
+    return lax.dot_general(a, b, (((1,), (0,)), ((), ())), preferred_element_type=F32)
+
+
+def exact_matmul(a, b):
+    return lax.dot_general(a, b, (((1,), (0,)), ((), ())), precision=lax.Precision.HIGHEST,
+                           preferred_element_type=F32)
+
+
+def solve_body(parts, basis, out, upper, raw):
     total = parts[0]
     for i in range(1, parts.shape[0]):
         total = total + parts[i]
@@ -335,48 +370,64 @@
     mirror = flipped[0:32]
     for b in range(1, 4):
         mirror = jnp.where(block == b, flipped[32 * b:32 * b + 32], mirror)
-    odd = jnp.where(within >= row, half, mirror)
-    even = jnp.where(within < row, half, jnp.where(within > row, mirror, jnp.broadcast_to(total[32:33], (32, NC))))
-
-    def pick(a, b, c, d):
-        return jnp.where(block == 0, a, jnp.where(block == 1, b, jnp.where(block == 2, c, d)))
-
-    odd_up, odd_down, even_up, even_down = turn(odd, 32), turn(odd, -32), turn(even, 32), turn(even, -32)
+    project = jnp.where(within >= row, half, mirror)
+    later = jnp.where(within < row, half, jnp.where(within > row, mirror, jnp.broadcast_to(total[32:33], (32, NC))))
+    early = project + 2.0 * turn(project, 32)
     gram = [
-        pick(even, odd, even_up, odd_up),
-        pick(odd_down, even, odd, even_up),
-        pick(even_down, odd_down, even, odd),
-        pick(turn(odd, -64), even_down, odd_down, even),
+        jnp.where(block == 3, turn(later, -32), turn(early, -32)),
+        jnp.where(block < 2, turn(early, 64), turn(later, 64)),
+        jnp.where(block < 1, turn(early, 32), turn(later, 32)),
+        later,
     ]
-    first = jnp.where(lane < 32, odd, 0.0)
-    second = jnp.where(lane < 32, even, 0.0) - 2.0 * first
-    third = jnp.where(lane < 32, odd_down, 0.0) - 2.0 * second
-    fourth = jnp.where(lane < 32, even_down, 0.0) - 2.0 * third
-    right = [first, second, third, fourth]
+    right = [jnp.where(lane < 32, turn(project, -32 * b), 0.0) for b in range(4)]
     g = [gram[t // 4][8 * (t % 4):8 * (t % 4) + 8] for t in range(16)]
     p = [right[t // 4][8 * (t % 4):8 * (t % 4) + 8] for t in range(16)]
     lane = lanes((8, NC))
     sub = lax.broadcasted_iota(jnp.int32, (8, NC), 0)
-    for k in range(128):
-        t, j = divmod(k, 8)
-        u = jnp.broadcast_to(g[t][j:j + 1, :], (8, NC))
-        up = jnp.broadcast_to(p[t][j:j + 1, :], (8, NC))
-        d = jnp.broadcast_to(u[:, k:k + 1], (8, NC))
-        inverse = 1.0 / d
-        line = jnp.where(lane >= k, u / jnp.sqrt(d), 0.0)
-        upper[k:k + 1, :] = line[0:1]
-        for i in range(16):
-            m = jnp.broadcast_to(g[i][:, k:k + 1], (8, NC)) * inverse
-            if i == t:
-                g[i] = jnp.where(sub == j, g[i] * inverse, g[i] - m * u)
-                p[i] = jnp.where(sub == j, p[i] * inverse, p[i] - m * up)
-            else:
-                g[i] = g[i] - m * u
-                p[i] = p[i] - m * up
-    weights = jnp.transpose(jnp.concatenate(p, axis=0))[0:32]
-    for r in range(NR):
-        moved = jnp.dot(weights, basis[r, 32:160, :], precision=lax.Precision.HIGHEST, preferred_element_type=F32)
-        out[pl.ds(r, 32, stride=NR), :] = basis[r, 0:32, :] - moved
+
+    def panel(first):
+        for k in range(8 * first, 8 * first + 64):
+            t, j = divmod(k, 8)
+            cols = {i: jnp.broadcast_to(g[i][:, k:k + 1], (8, NC)) for i in range(first, first + 8)}
+            inverse = 1.0 / jnp.broadcast_to(cols[t][j:j + 1, :], (8, NC))
+            raw[k:k + 1, :] = g[t][j:j + 1, :]
+            u = jnp.broadcast_to(g[t][j:j + 1, :], (8, NC)) * inverse
+            up = jnp.broadcast_to(p[t][j:j + 1, :], (8, NC)) * inverse
+            cols[t] = jnp.where(sub == j, 0.0, cols[t])
+            for i in range(first, first + 8):
+                g[i] = g[i] - cols[i] * u
+                p[i] = p[i] - cols[i] * up
+        for t in range(first, first + 8):
+            line = raw[8 * t:8 * t + 8, :]
+            diagonal = jnp.sum(jnp.where(lane == sub + 8 * t, line, 0.0), axis=1, keepdims=True)
+            diagonal = jnp.broadcast_to(diagonal, (8, NC))
+            upper[8 * t:8 * t + 8, :] = jnp.where(lane >= sub + 8 * t, line / jnp.sqrt(diagonal), 0.0)
+            inverse = 1.0 / diagonal
+            g[t] = g[t] * inverse
+            p[t] = p[t] * inverse
+
+    below = jnp.concatenate(g[8:16], axis=0)[:, 0:64]
+    panel(0)
+    scaled = jnp.concatenate([jnp.concatenate(g[0:8], axis=0), jnp.concatenate(p[0:8], axis=0)], axis=1)
+    update = exact_matmul(below, scaled)
+    for t in range(8, 16):
+        g[t] = g[t] - update[8 * t - 64:8 * t - 56, 0:NC]
+        p[t] = p[t] - update[8 * t - 64:8 * t - 56, NC:]
+    panel(8)
+    last = jnp.concatenate(p[8:16], axis=0)
+    above = turn(scaled[:, 0:NC], 64)[:, 0:64]
+    first = scaled[:, NC:] - exact_matmul(above, last)
+    weights = jnp.transpose(jnp.concatenate([first, last], axis=0))[0:32]
+    high, mid, low = split(weights)
+    left_a = jnp.concatenate([jnp.concatenate([high, high], axis=1), jnp.concatenate([mid, mid], axis=1)], axis=0)
+    left_b = jnp.concatenate([high, low], axis=1)
+    for r in range(0, NR, 2):
+        w_high, w_mid, w_low = split(jnp.concatenate([basis[r, 32:160, :], basis[r + 1, 32:160, :]], axis=1))
+        moved_a = matmul(left_a, jnp.concatenate([w_high, w_mid], axis=0))
+        moved_b = matmul(left_b, jnp.concatenate([w_low, w_high], axis=0))
+        moved = moved_a[0:32] + (moved_a[32:64] + moved_b)
+        out[pl.ds(r, 32, stride=NR), :] = basis[r, 0:32, :] - moved[:, :NC]
+        out[pl.ds(r + 1, 32, stride=NR), :] = basis[r + 1, 0:32, :] - moved[:, NC:]
 
 
 def shape(*dims):
@@ -423,8 +474,11 @@
         scratch=[
             pltpu.VMEM((NCOEF, 40, NC), F32),
             pltpu.VMEM((NCOEF, 40, NC), F32),
-            pltpu.VMEM((4, 36, 40, NC), F32),
-            pltpu.VMEM((160, NC), F32),
+            pltpu.VMEM((36, 40, NC), F32),
+            pltpu.VMEM((36, 40, NC), F32),
+            pltpu.VMEM((36, 40, NC), F32),
+            pltpu.VMEM((36, 40, NC), F32),
+            pltpu.VMEM((96, NC), F32),
         ],
         name="products",
     )(ini_x, src_x, w_main, w_strip, from_up, from_down)
@@ -438,6 +492,7 @@
     new_residual, upper = call(
         solve_body,
         (shape(NF * NR, NC), shape(128, 128)),
+        scratch=[pltpu.VMEM((128, NC), F32)],
         name="solve",
     )(gathered, basis)
     return (new_residual.reshape(NF, NR, NC), upper)

time: 119 us -> 106 us (0.89)
  Pallas kernels: 55.5 us -> 42.5 us
    pallas_call x1, Pallas kernels: 27.9 us -> 15.1 us  [on_device(): call(products, (shape(NR, 160, NC), shape(40, NC)), scratch=[pltpu.VMEM((...]
where the time goes in v2:
time: 106 us; the launch traced here: 105 us
  Pallas kernels  42.5 us (40%)
  blocking collectives  32.9 us (31%)
  waiting for transfers between devices  14.2 us (13%)
  starting transfers between devices  12.3 us (12%)
  local copies, waits for them, and re-layouts  1.48 us (1%)
  other arithmetic  1.38 us (1%)
    all_to_all x2, blocking collectives, on_device(): lax.all_to_all(jnp.broadcast_to(packed[None], (count, 40, NC)), axes, 0, 0)  32.9 us
    pallas_call x1, Pallas kernels, on_device(): call(solve_body, (shape(NF * NR, NC), shape(128, 128)), scratch=[pltpu.VM...  20.5 us
    pallas_call x1, Pallas kernels, on_device(): call(products, (shape(NR, 160, NC), shape(40, NC)), scratch=[pltpu.VMEM((...  15.1 us
    ppermute x1, starting transfers between devices, on_device(): from_up = lax.ppermute(to_down, dom, neighbours(dom_count, 1))  5.1 us
    ppermute x1, waiting for transfers between devices, on_device(): from_up = lax.ppermute(to_down, dom, neighbours(dom_count, 1))  4.32 us
    ppermute x1, waiting for transfers between devices, on_device(): from_down = lax.ppermute(to_up, dom, neighbours(dom_count, -1))  4.29 us
    ppermute x1, starting transfers between devices, on_device(): from_left = lax.ppermute(to_right, sub, neighbours(sub_count, 1))  4.01 us
    pallas_call x1, Pallas kernels, on_device(): call(prepare, (shape(NR, 40, NC), shape(NR, 40, NC), shape(NH, 24, NC), s...  3.8 us
  transfers between devices with their start and end apart: 5, of which 5 were waited for; matrix products, arithmetic and copies ran while one was open for 0% of the time, Pallas kernels for 0%

profile of v2, /device:TPU:1, one launch (start us, length us, event | category | flops | bytes accessed | tf_op | source)
XLA Modules:
  0.0 105.5 jit_solution(15882150986980942617)
XLA Ops:
  0.6 0.6 pad_add_fusion.refs_0_
  1.3 3.8 %prepare.1 = (f32[16,40,128]{2,1,0:T(8,128)}, f32[16,40,128]{2,1,0:T(8,128)}, f32[13,24,128]{2,1,0:T(8,128)}, f32[4,24,128]{2,1,0:T(8,128)}, f32[176,128]{1,0:T(8,128)}, /*index=5*/f32[176,128]{1,0:T(8,128)}) custom-call(s32[2]{0:T(128)} %pad_add_fusion.refs_0_, f32[512,128]{1,0:T(8,128)} %bitcast.7, f32[512,128]{1,0:T(8,128)} %bitcast.8, ...), custom_call_target="tpu_custom_call" | custom-call | tf_op jit(solution)/shard_map/prepare/pallas_call | solution.py:448
  5.1 4.0 %collective-permute-start = (f32[176,128]{1,0:T(8,128)}, f32[176,128]{1,0:T(8,128)S(1)}, u32[]{:S(2)}, u32[]{:S(2)}) collective-permute-start(f32[176,128]{1,0:T(8,128)} %get-tuple-element.22), channel_id=1, source_target_pairs={{0,1},{1,2},{2,3},{4,5},{5,6},{6,7},{8,9},{9,10},{10,11},{12,13},{... | collective-permute-start | bytes 270344 | tf_op jit(solution)/shard_map/ppermute | solution.py:458
  9.1 1.3 %collective-permute-start.1 = (f32[176,128]{1,0:T(8,128)}, f32[176,128]{1,0:T(8,128)S(1)}, u32[]{:S(2)}, u32[]{:S(2)}) collective-permute-start(f32[176,128]{1,0:T(8,128)} %get-tuple-element.23), channel_id=1, source_target_pairs={{1,0},{2,1},{3,2},{5,4},{6,5},{7,6},{9,8},{10,9},{11,10},{13,12},{... | collective-permute-start | bytes 270344 | tf_op jit(solution)/shard_map/ppermute | solution.py:457
  10.4 0.6 collective-permute-done.from_left
  10.9 0.0 copy-start.2
  10.9 3.6 %collective-permute-done.1.from_right = f32[176,128]{1,0:T(8,128)S(1)} collective-permute-done((f32[176,128]{1,0:T(8,128)}, f32[176,128]{1,0:T(8,128)S(1)}, u32[]{:S(2)}, u32[]{:S(2)}) %collective-permute-start.1) | collective-permute-done | bytes 90144 | tf_op jit(solution)/shard_map/ppermute | solution.py:457
  14.6 0.0 copy-start.3
  14.6 0.0 copy-done.2
  14.6 0.6 copy-done.3
  15.2 3.1 %columns.1 = (f32[16,40,128]{2,1,0:T(8,128)}, f32[16,40,128]{2,1,0:T(8,128)}, f32[13,24,128]{2,1,0:T(8,128)}, f32[4,24,128]{2,1,0:T(8,128)}, f32[992,128]{1,0:T(8,128)}, /*index=5*/f32[992,128]{1,0:T(8,128)}) custom-call(f32[16,40,128]{2,1,0:T(8,128)} %get-tuple-element.18.ini_x, f32[16,40,128]{2,1,0:T(8,128)} %get-tuple-element.19.src_x, ...), custom_call_target="tpu_custom_call" | custom-call | tf_op jit(solution)/shard_map/columns/pallas_call | solution.py:459
  18.3 5.1 %collective-permute-start.2 = (f32[992,128]{1,0:T(8,128)}, f32[992,128]{1,0:T(8,128)S(1)}, u32[]{:S(2)}, u32[]{:S(2)}) collective-permute-start(f32[992,128]{1,0:T(8,128)} %get-tuple-element.28), channel_id=1, source_target_pairs={{0,4},{4,8},{8,12},{12,16},{16,20},{20,24},{24,28},{28,32},{32,36}... | collective-permute-start | bytes 1523720 | tf_op jit(solution)/shard_map/ppermute | solution.py:466
  23.4 1.9 %collective-permute-start.3 = (f32[992,128]{1,0:T(8,128)}, f32[992,128]{1,0:T(8,128)S(1)}, u32[]{:S(2)}, u32[]{:S(2)}) collective-permute-start(f32[992,128]{1,0:T(8,128)} %get-tuple-element.29), channel_id=1, source_target_pairs={{4,0},{8,4},{12,8},{16,12},{20,16},{24,20},{28,24},{32,28},{36,32}... | collective-permute-start | bytes 1523720 | tf_op jit(solution)/shard_map/ppermute | solution.py:465
  25.3 4.3 %collective-permute-done.2.refs_4_ = f32[992,128]{1,0:T(8,128)S(1)} collective-permute-done((f32[992,128]{1,0:T(8,128)}, f32[992,128]{1,0:T(8,128)S(1)}, u32[]{:S(2)}, u32[]{:S(2)}) %collective-permute-start.2) | collective-permute-done | bytes 507936 | tf_op jit(solution)/shard_map/ppermute | solution.py:466
  29.7 0.0 copy-start
  29.7 4.3 %collective-permute-done.3.refs_5_ = f32[992,128]{1,0:T(8,128)S(1)} collective-permute-done((f32[992,128]{1,0:T(8,128)}, f32[992,128]{1,0:T(8,128)S(1)}, u32[]{:S(2)}, u32[]{:S(2)}) %collective-permute-start.3) | collective-permute-done | bytes 507936 | tf_op jit(solution)/shard_map/ppermute | solution.py:465
  34.0 0.0 copy-start.1
  34.0 0.0 copy-done
  34.0 0.8 copy-done.1
  34.8 15.1 %products.1 = (f32[16,160,128]{2,1,0:T(8,128)}, f32[40,128]{1,0:T(8,128)}) custom-call(f32[16,40,128]{2,1,0:T(8,128)} %get-tuple-element.24.refs_0_, f32[16,40,128]{2,1,0:T(8,128)} %get-tuple-element.25.refs_1_, f32[13,24,128]{2,1,0:T(8,128)} %get-tuple-element.26.refs_2_, f32[4,24,128]{2,1,0:T(8,128)} %get-tuple-element.27.refs_3_, f32[992,128]{1,0:T(8,128)} %copy-done, ...), custom_call_target="tpu_custom_call" | custom-call | tf_op jit(solution)/shard_map/products/pallas_call | solution.py:471
  49.9 0.0 collective-permute-start.4
  49.9 1.4 %collective-permute-done.4 = f32[40,128]{1,0:T(8,128)S(1)} collective-permute-done((f32[40,128]{1,0:T(8,128)}, f32[40,128]{1,0:T(8,128)S(1)}, u32[]{:S(2)}, u32[]{:S(2)}) %collective-permute-start.4) | collective-permute-done | bytes 20512 | tf_op jit(solution)/shard_map/ppermute | solution.py:487
  51.3 0.7 reduce_sum.17
  52.1 16.6 %all_to_all.10 = f32[16,40,128]{2,1,0:T(8,128)S(1)} all-to-all(f32[16,40,128]{2,1,0:T(8,128)S(1)} %broadcast_in_dim.4), channel_id=1, replica_groups=mesh['z'=8,'x'=4,'c'=2,'sub'=4] {'x','sub'}, dimensions={0} | all-to-all | bytes 655360 | tf_op jit(solution)/shard_map/all_to_all | solution.py:489
  68.7 16.3 %all_to_all.11.parts = f32[8,40,128]{2,1,0:T(8,128)} all-to-all(f32[8,40,128]{2,1,0:T(8,128)S(1)} %broadcast_in_dim.5), channel_id=1, replica_groups=mesh['z'=8,'x'=4,'c'=2,'sub'=4] {'z'}, dimensions={0} | all-to-all | bytes 327680 | tf_op jit(solution)/shard_map/all_to_all | solution.py:489
  85.0 20.5 %solve.1 = (f32[512,128]{1,0:T(8,128)}, f32[128,128]{1,0:T(8,128)}) custom-call(f32[8,40,128]{2,1,0:T(8,128)} %all_to_all.11.parts, f32[16,160,128]{2,1,0:T(8,128)} %get-tuple-element.31.basis), custom_call_target="tpu_custom_call" | custom-call | tf_op jit(solution)/shard_map/solve/pallas_call | solution.py:492
  (3 shorter events, 0.1 us)
Async XLA Ops:
  5.1 5.9 %collective-permute-start = (f32[176,128]{1,0:T(8,128)}, f32[176,128]{1,0:T(8,128)S(1)}, u32[]{:S(2)}, u32[]{:S(2)}) collective-permute-start(f32[176,128]{1,0:T(8,128)} %get-tuple-element.22), channel_id=1, source_target_pairs={{0,1},{1,2},{2,3},{4,5},{5,6},{6,7},{8,9},{9,10},{10,11},{12,13},{... | collective-permute-start | bytes 270344 | tf_op jit(solution)/shard_map/ppermute | solution.py:458
  9.1 5.5 %collective-permute-start.1 = (f32[176,128]{1,0:T(8,128)}, f32[176,128]{1,0:T(8,128)S(1)}, u32[]{:S(2)}, u32[]{:S(2)}) collective-permute-start(f32[176,128]{1,0:T(8,128)} %get-tuple-element.23), channel_id=1, source_target_pairs={{1,0},{2,1},{3,2},{5,4},{6,5},{7,6},{9,8},{10,9},{11,10},{13,12},{... | collective-permute-start | bytes 270344 | tf_op jit(solution)/shard_map/ppermute | solution.py:457
  10.9 3.6 %copy-start.2 = (f32[176,128]{1,0:T(8,128)}, f32[176,128]{1,0:T(8,128)S(1)}, u32[]{:S(2)}) copy-start(f32[176,128]{1,0:T(8,128)S(1)} %collective-permute-done.from_left) | copy-start | bytes 270340
  14.6 0.6 copy-start.3
  18.3 11.3 %collective-permute-start.2 = (f32[992,128]{1,0:T(8,128)}, f32[992,128]{1,0:T(8,128)S(1)}, u32[]{:S(2)}, u32[]{:S(2)}) collective-permute-start(f32[992,128]{1,0:T(8,128)} %get-tuple-element.28), channel_id=1, source_target_pairs={{0,4},{4,8},{8,12},{12,16},{16,20},{20,24},{24,28},{28,32},{32,36}... | collective-permute-start | bytes 1523720 | tf_op jit(solution)/shard_map/ppermute | solution.py:466
  23.4 10.5 %collective-permute-start.3 = (f32[992,128]{1,0:T(8,128)}, f32[992,128]{1,0:T(8,128)S(1)}, u32[]{:S(2)}, u32[]{:S(2)}) collective-permute-start(f32[992,128]{1,0:T(8,128)} %get-tuple-element.29), channel_id=1, source_target_pairs={{4,0},{8,4},{12,8},{16,12},{20,16},{24,20},{28,24},{32,28},{36,32}... | collective-permute-start | bytes 1523720 | tf_op jit(solution)/shard_map/ppermute | solution.py:465
  29.7 4.3 %copy-start = (f32[992,128]{1,0:T(8,128)}, f32[992,128]{1,0:T(8,128)S(1)}, u32[]{:S(2)}) copy-start(f32[992,128]{1,0:T(8,128)S(1)} %collective-permute-done.2.refs_4_) | copy-start | bytes 1523716
  34.0 0.8 copy-start.1
  49.9 1.4 %collective-permute-start.4 = (f32[40,128]{1,0:T(8,128)}, f32[40,128]{1,0:T(8,128)S(1)}, u32[]{:S(2)}, u32[]{:S(2)}) collective-permute-start(f32[40,128]{1,0:T(8,128)} %get-tuple-element.30), channel_id=1, source_target_pairs={{0,4},{4,0},{1,5},{5,1},{2,6},{6,2},{3,7},{7,3},{8,12},{12,8},{9,1... | collective-permute-start | bytes 61448 | tf_op jit(solution)/shard_map/ppermute | solution.py:487

commit v3 on v2

--- a/solution.py
+++ b/solution.py
@@ -37,18 +37,21 @@
         out_shape=outs,
         scratch_shapes=scratch,
         interpret=INTERPRET,
+        compiler_params=pltpu.CompilerParams(vmem_limit_bytes=16 << 20),
         **kw,
     )
 
 
-def vmem_specs(count):
-    return [pl.BlockSpec(memory_space=pltpu.VMEM)] * count
-
-
-def prepare_body(rows_total, cols_total, pos, source, initial, mass, slots, stiffness,
+def near(*values):
+    if INTERPRET:
+        return values
+    return tuple(pltpu.with_memory_space_constraint(v, pltpu.VMEM) for v in values)
+
+
+def prepare_body(dom, sub_axis, rows_total, cols_total, source, initial, mass, slots, stiffness,
                  ini_x, src_x, w_main, w_strip, to_left, to_right, acc):
-    row = lax.broadcasted_iota(jnp.int32, (NR, NC), 0) + pos[0] * NR
-    col = lanes((NR, NC)) + pos[1] * NC
+    row = lax.broadcasted_iota(jnp.int32, (NR, NC), 0) + lax.axis_index(dom) * NR
+    col = lanes((NR, NC)) + lax.axis_index(sub_axis) * NC
     top, bottom = row == 0, row == rows_total - 1
     west, east = col == 0, col == cols_total - 1
     kept = []
@@ -385,18 +388,37 @@
     lane = lanes((8, NC))
     sub = lax.broadcasted_iota(jnp.int32, (8, NC), 0)
 
+    def spread(value, j):
+        return jnp.broadcast_to(value[j:j + 1, :], (8, NC))
+
+    def columns(value, base):
+        return [jnp.broadcast_to(value[:, base + q:base + q + 1], (8, NC)) for q in range(8)]
+
     def panel(first):
-        for k in range(8 * first, 8 * first + 64):
-            t, j = divmod(k, 8)
-            cols = {i: jnp.broadcast_to(g[i][:, k:k + 1], (8, NC)) for i in range(first, first + 8)}
-            inverse = 1.0 / jnp.broadcast_to(cols[t][j:j + 1, :], (8, NC))
-            raw[k:k + 1, :] = g[t][j:j + 1, :]
-            u = jnp.broadcast_to(g[t][j:j + 1, :], (8, NC)) * inverse
-            up = jnp.broadcast_to(p[t][j:j + 1, :], (8, NC)) * inverse
-            cols[t] = jnp.where(sub == j, 0.0, cols[t])
-            for i in range(first, first + 8):
-                g[i] = g[i] - cols[i] * u
-                p[i] = p[i] - cols[i] * up
+        for t in range(first, first + 8):
+            col = columns(g[t], 8 * t)
+            steps = []
+            for j in range(8):
+                inverse = 1.0 / spread(col[j], j)
+                raw[8 * t + j:8 * t + j + 1, :] = g[t][j:j + 1, :]
+                u = spread(g[t], j) * inverse
+                up = spread(p[t], j) * inverse
+                m = jnp.where(sub == j, 0.0, col[j])
+                scaled_cols = {}
+                for q in range(j + 1, 8):
+                    scaled_cols[q] = spread(col[q], j) * inverse
+                    col[q] = col[q] - m * scaled_cols[q]
+                g[t] = g[t] - m * u
+                p[t] = p[t] - m * up
+                steps.append((scaled_cols, u, up))
+            for i in [first + (t - first + n) % 8 for n in range(1, 8)]:
+                col = columns(g[i], 8 * t)
+                for j in range(8):
+                    scaled_cols, u, up = steps[j]
+                    for q in range(j + 1, 8):
+                        col[q] = col[q] - col[j] * scaled_cols[q]
+                    g[i] = g[i] - col[j] * u
+                    p[i] = p[i] - col[j] * up
         for t in range(first, first + 8):
             line = raw[8 * t:8 * t + 8, :]
             diagonal = jnp.sum(jnp.where(lane == sub + 8 * t, line, 0.0), axis=1, keepdims=True)
@@ -430,8 +452,12 @@
         out[pl.ds(r + 1, 32, stride=NR), :] = basis[r + 1, 0:32, :] - moved[:, NC:]
 
 
+def far(*dims):
+    return jax.ShapeDtypeStruct(dims, F32)
+
+
 def shape(*dims):
-    return jax.ShapeDtypeStruct(dims, F32)
+    return far(*dims) if INTERPRET else pltpu.VMEM(dims, F32)
 
 
 def neighbours(count, step):
@@ -440,19 +466,16 @@
 
 def on_device(dom, sub, dom_count, sub_count, reduce_groups, source, initial, lumped_mass, node_slots, stiffness):
     rows_total, cols_total = dom_count * NR, sub_count * NC
-    pos = jnp.stack([lax.axis_index(dom), lax.axis_index(sub)]).astype(jnp.int32)
 
     def prepare(*refs):
-        prepare_body(rows_total, cols_total, *refs)
+        prepare_body(dom, sub, rows_total, cols_total, *refs)
 
     ini_x, src_x, w_main, w_strip, to_left, to_right = call(
         prepare,
         (shape(NR, 40, NC), shape(NR, 40, NC), shape(NH, 24, NC), shape(4, 24, NC), shape(176, NC), shape(176, NC)),
         scratch=[pltpu.VMEM((3, NH, 24, NC), F32)],
-        in_specs=[pl.BlockSpec(memory_space=pltpu.SMEM)] + vmem_specs(5),
-        out_specs=tuple(vmem_specs(6)),
         name="prepare",
-    )(pos, source.reshape(NF * NR, NC), initial.reshape(NF * NR, NC), lumped_mass, node_slots,
+    )(source.reshape(NF * NR, NC), initial.reshape(NF * NR, NC), lumped_mass, node_slots,
       stiffness.reshape(36, NR, NC))
     from_right = lax.ppermute(to_left, sub, neighbours(sub_count, -1))
     from_left = lax.ppermute(to_right, sub, neighbours(sub_count, 1))
@@ -461,7 +484,7 @@
         (shape(NR, 40, NC), shape(NR, 40, NC), shape(NH, 24, NC), shape(4, 24, NC), shape(ROW_END, NC),
          shape(ROW_END, NC)),
         name="columns",
-    )(ini_x, src_x, w_main, w_strip, from_left, from_right)
+    )(*near(ini_x, src_x, w_main, w_strip, from_left, from_right))
     from_down = lax.ppermute(to_up, dom, neighbours(dom_count, -1))
     from_up = lax.ppermute(to_down, dom, neighbours(dom_count, 1))
 
@@ -481,7 +504,7 @@
             pltpu.VMEM((96, NC), F32),
         ],
         name="products",
-    )(ini_x, src_x, w_main, w_strip, from_up, from_down)
+    )(*near(ini_x, src_x, w_main, w_strip, from_up, from_down))
     for i, (axes, count) in enumerate(reduce_groups):
         if count == 2:
             gathered = jnp.stack([packed, lax.ppermute(packed, axes, [(0, 1), (1, 0)])])
@@ -491,10 +514,10 @@
             packed = jnp.sum(gathered, axis=0)
     new_residual, upper = call(
         solve_body,
-        (shape(NF * NR, NC), shape(128, 128)),
+        (far(NF * NR, NC), far(128, 128)),
         scratch=[pltpu.VMEM((128, NC), F32)],
         name="solve",
-    )(gathered, basis)
+    )(*near(gathered, basis))
     return (new_residual.reshape(NF, NR, NC), upper)
 
 

time: 106 us -> 86.8 us (0.82)
  Pallas kernels: 42.5 us -> 21.9 us
  local copies, waits for them, and re-layouts: 1.48 us -> 4.39 us
  other arithmetic: 1.38 us -> 0.03 us
    pallas_call x1, Pallas kernels: 20.5 us -> 6.52 us  [on_device(): call(solve_body, (far(NF * NR, NC), far(128, 128)), scratch=[pltpu.VMEM((...]
    unnamed x8 -> x10, local copies, waits for them, and re-layouts: 1.44 us -> 4.35 us
    pallas_call x1, Pallas kernels: 3.11 us -> 0.74 us  [on_device(): call(columns_body, (shape(NR, 40, NC), shape(NR, 40, NC), shape(NH, 24, N...]
    pallas_call x1, Pallas kernels: 15.1 us -> 12.9 us  [on_device(): call(products, (shape(NR, 160, NC), shape(40, NC)), scratch=[pltpu.VMEM((...]
    pallas_call x1, Pallas kernels: 3.8 us -> 1.68 us  [on_device(): call(prepare, (shape(NR, 40, NC), shape(NR, 40, NC), shape(NH, 24, NC), s...]
where the time goes in v3:
time: 86.8 us; the launch traced here: 85.8 us
  blocking collectives  32.8 us (38%)
  Pallas kernels  21.9 us (25%)
  waiting for transfers between devices  13.5 us (16%)
  starting transfers between devices  12.4 us (14%)
  local copies, waits for them, and re-layouts  4.39 us (5%)
    all_to_all x2, blocking collectives, on_device(): lax.all_to_all(jnp.broadcast_to(packed[None], (count, 40, NC)), axes, 0, 0)  32.8 us
    pallas_call x1, Pallas kernels, on_device(): call(products, (shape(NR, 160, NC), shape(40, NC)), scratch=[pltpu.VMEM((...  12.9 us
    pallas_call x1, Pallas kernels, on_device(): call(solve_body, (far(NF * NR, NC), far(128, 128)), scratch=[pltpu.VMEM((...  6.52 us
    ppermute x1, starting transfers between devices, on_device(): from_up = lax.ppermute(to_down, dom, neighbours(dom_count, 1))  5.11 us
    ppermute x1, waiting for transfers between devices, on_device(): from_down = lax.ppermute(to_up, dom, neighbours(dom_count, -1))  4.4 us
    unnamed x10, local copies, waits for them, and re-layouts  4.35 us
    ppermute x1, starting transfers between devices, on_device(): from_left = lax.ppermute(to_right, sub, neighbours(sub_count, 1))  4.02 us
    ppermute x1, waiting for transfers between devices, on_device(): from_up = lax.ppermute(to_down, dom, neighbours(dom_count, 1))  4 us
  transfers between devices with their start and end apart: 5, of which 5 were waited for; matrix products, arithmetic and copies ran while one was open for 0% of the time, Pallas kernels for 0%

profile of v3, /device:TPU:1, one launch (start us, length us, event | category | flops | bytes accessed | tf_op | source)
XLA Modules:
  0.0 85.8 jit_solution(10755299303860005035)
XLA Ops:
  0.6 0.0 copy-start
  0.6 1.0 %copy-done = f32[6,6,16,128]{3,2,1,0:T(8,128)S(1)} copy-done((f32[6,6,16,128]{3,2,1,0:T(8,128)S(1)}, f32[6,6,16,128]{3,2,1,0:T(8,128)}, u32[]{:S(2)}) %copy-start) | copy-done | bytes 294936
  1.6 0.0 copy-start.1
  1.6 0.9 %copy-done.1 = f32[32,16,128]{2,1,0:T(8,128)S(1)} copy-done((f32[32,16,128]{2,1,0:T(8,128)S(1)}, f32[32,16,128]{2,1,0:T(8,128)}, u32[]{:S(2)}) %copy-start.1) | copy-done | bytes 262168
  2.5 0.0 copy-start.2
  2.5 0.9 %copy-done.2 = f32[32,16,128]{2,1,0:T(8,128)S(1)} copy-done((f32[32,16,128]{2,1,0:T(8,128)S(1)}, f32[32,16,128]{2,1,0:T(8,128)}, u32[]{:S(2)}) %copy-start.2) | copy-done | bytes 262168
  3.5 0.0 copy-start.3
  3.5 0.8 copy-done.3
  4.3 0.0 copy-start.4
  4.3 0.7 copy-done.4
  5.0 1.7 %prepare.1 = (f32[16,40,128]{2,1,0:T(8,128)S(1)}, f32[16,40,128]{2,1,0:T(8,128)S(1)}, f32[13,24,128]{2,1,0:T(8,128)S(1)}, f32[4,24,128]{2,1,0:T(8,128)S(1)}, f32...) custom-call(f32[512,128]{1,0:T(8,128)S(1)} %bitcast.5, f32[512,128]{1,0:T(8,128)S(1)} %bitcast.6, f32[16,128]{1,0:T(8,128)S(1)} %copy-done.4, ...), custom_call_target="tpu_custom_call" | custom-call | tf_op jit(solution)/shard_map/prepare/pallas_call | solution.py:473
  6.7 4.0 %collective-permute-start = (f32[176,128]{1,0:T(8,128)S(1)}, f32[176,128]{1,0:T(8,128)S(1)}, u32[]{:S(2)}, u32[]{:S(2)}) collective-permute-start(f32[176,128]{1,0:T(8,128)S(1)} %get-tuple-element.22), channel_id=1, source_target_pairs={{0,1},{1,2},{2,3},{4,5},{5,6},{6,7},{8,9},{9,10},{10,11},{12,13},{... | collective-permute-start | bytes 270344 | tf_op jit(solution)/shard_map/ppermute | solution.py:481
  10.7 1.3 %collective-permute-start.1 = (f32[176,128]{1,0:T(8,128)S(1)}, f32[176,128]{1,0:T(8,128)S(1)}, u32[]{:S(2)}, u32[]{:S(2)}) collective-permute-start(f32[176,128]{1,0:T(8,128)S(1)} %get-tuple-element.23), channel_id=1, source_target_pairs={{1,0},{2,1},{3,2},{5,4},{6,5},{7,6},{9,8},{10,9},{11,10},{13,12},{... | collective-permute-start | bytes 270344 | tf_op jit(solution)/shard_map/ppermute | solution.py:480
  12.0 0.2 collective-permute-done.from_left
  12.2 3.7 %collective-permute-done.1.from_right = f32[176,128]{1,0:T(8,128)S(1)} collective-permute-done((f32[176,128]{1,0:T(8,128)S(1)}, f32[176,128]{1,0:T(8,128)S(1)}, u32[]{:S(2)}, u32[]{:S(2)}) %collective-permute-start.1) | collective-permute-done | bytes 90144 | tf_op jit(solution)/shard_map/ppermute | solution.py:480
  16.0 0.7 columns.1
  16.7 5.1 %collective-permute-start.2 = (f32[992,128]{1,0:T(8,128)S(1)}, f32[992,128]{1,0:T(8,128)S(1)}, u32[]{:S(2)}, u32[]{:S(2)}) collective-permute-start(f32[992,128]{1,0:T(8,128)S(1)} %get-tuple-element.28), channel_id=1, source_target_pairs={{0,4},{4,8},{8,12},{12,16},{16,20},{20,24},{24,28},{28,32},{32,36}... | collective-permute-start | bytes 1523720 | tf_op jit(solution)/shard_map/ppermute | solution.py:489
  21.8 1.9 %collective-permute-start.3 = (f32[992,128]{1,0:T(8,128)S(1)}, f32[992,128]{1,0:T(8,128)S(1)}, u32[]{:S(2)}, u32[]{:S(2)}) collective-permute-start(f32[992,128]{1,0:T(8,128)S(1)} %get-tuple-element.29), channel_id=1, source_target_pairs={{4,0},{8,4},{12,8},{16,12},{20,16},{24,20},{28,24},{32,28},{36,32}... | collective-permute-start | bytes 1523720 | tf_op jit(solution)/shard_map/ppermute | solution.py:488
  23.8 4.0 %collective-permute-done.2.refs_4_ = f32[992,128]{1,0:T(8,128)S(1)} collective-permute-done((f32[992,128]{1,0:T(8,128)S(1)}, f32[992,128]{1,0:T(8,128)S(1)}, u32[]{:S(2)}, u32[]{:S(2)}) %collective-permute-start.2) | collective-permute-done | bytes 507936 | tf_op jit(solution)/shard_map/ppermute | solution.py:489
  27.8 4.4 %collective-permute-done.3.refs_5_ = f32[992,128]{1,0:T(8,128)S(1)} collective-permute-done((f32[992,128]{1,0:T(8,128)S(1)}, f32[992,128]{1,0:T(8,128)S(1)}, u32[]{:S(2)}, u32[]{:S(2)}) %collective-permute-start.3) | collective-permute-done | bytes 507936 | tf_op jit(solution)/shard_map/ppermute | solution.py:488
  32.2 12.9 %products.1 = (f32[16,160,128]{2,1,0:T(8,128)S(1)}, f32[40,128]{1,0:T(8,128)S(1)}) custom-call(f32[16,40,128]{2,1,0:T(8,128)S(1)} %get-tuple-element.24.refs_0_, f32[16,40,128]{2,1,0:T(8,128)S(1)} %get-tuple-element.25.refs_1_, f32[13,24,128]{2,1,0:T(8,128)S(1)} %get-tuple-element.26.refs_2_, f32[4,24,128]{2,1,0:T(8,128)S(1)} %get-tuple-element.27.refs_3_, ...), custom_call_target="tpu_custom_call" | custom-call | tf_op jit(solution)/shard_map/products/pallas_call | solution.py:494
  45.1 0.1 collective-permute-start.4
  45.2 1.2 %collective-permute-done.4 = f32[40,128]{1,0:T(8,128)S(1)} collective-permute-done((f32[40,128]{1,0:T(8,128)S(1)}, f32[40,128]{1,0:T(8,128)S(1)}, u32[]{:S(2)}, u32[]{:S(2)}) %collective-permute-start.4) | collective-permute-done | bytes 20512 | tf_op jit(solution)/shard_map/ppermute | solution.py:510
  46.4 16.6 %all_to_all.10 = f32[16,40,128]{2,1,0:T(8,128)S(1)} all-to-all(f32[16,40,128]{2,1,0:T(8,128)S(1)} %broadcast_in_dim.4), channel_id=1, replica_groups=mesh['z'=8,'x'=4,'c'=2,'sub'=4] {'x','sub'}, dimensions={0} | all-to-all | bytes 655360 | tf_op jit(solution)/shard_map/all_to_all | solution.py:512
  63.1 16.2 %all_to_all.11.parts = f32[8,40,128]{2,1,0:T(8,128)S(1)} all-to-all(f32[8,40,128]{2,1,0:T(8,128)S(1)} %broadcast_in_dim.5), channel_id=1, replica_groups=mesh['z'=8,'x'=4,'c'=2,'sub'=4] {'z'}, dimensions={0} | all-to-all | bytes 327680 | tf_op jit(solution)/shard_map/all_to_all | solution.py:512
  79.3 6.5 %solve.1 = (f32[512,128]{1,0:T(8,128)}, f32[128,128]{1,0:T(8,128)}) custom-call(f32[8,40,128]{2,1,0:T(8,128)S(1)} %all_to_all.11.parts, f32[16,160,128]{2,1,0:T(8,128)S(1)} %get-tuple-element.31.basis), custom_call_target="tpu_custom_call" | custom-call | tf_op jit(solution)/shard_map/solve/pallas_call | solution.py:515
  (4 shorter events, 0.1 us)
Async XLA Ops:
  0.6 1.0 %copy-start = (f32[6,6,16,128]{3,2,1,0:T(8,128)S(1)}, f32[6,6,16,128]{3,2,1,0:T(8,128)}, u32[]{:S(2)}) copy-start(f32[6,6,16,128]{3,2,1,0:T(8,128)} %param.9) | copy-start | bytes 884740
  1.6 0.9 %copy-start.1 = (f32[32,16,128]{2,1,0:T(8,128)S(1)}, f32[32,16,128]{2,1,0:T(8,128)}, u32[]{:S(2)}) copy-start(f32[32,16,128]{2,1,0:T(8,128)} %param.5) | copy-start | bytes 786436
  2.5 0.9 %copy-start.2 = (f32[32,16,128]{2,1,0:T(8,128)S(1)}, f32[32,16,128]{2,1,0:T(8,128)}, u32[]{:S(2)}) copy-start(f32[32,16,128]{2,1,0:T(8,128)} %param.6) | copy-start | bytes 786436
  3.5 0.8 copy-start.3
  4.3 0.7 copy-start.4
  6.7 5.6 %collective-permute-start = (f32[176,128]{1,0:T(8,128)S(1)}, f32[176,128]{1,0:T(8,128)S(1)}, u32[]{:S(2)}, u32[]{:S(2)}) collective-permute-start(f32[176,128]{1,0:T(8,128)S(1)} %get-tuple-element.22), channel_id=1, source_target_pairs={{0,1},{1,2},{2,3},{4,5},{5,6},{6,7},{8,9},{9,10},{10,11},{12,13},{... | collective-permute-start | bytes 270344 | tf_op jit(solution)/shard_map/ppermute | solution.py:481
  10.7 5.3 %collective-permute-start.1 = (f32[176,128]{1,0:T(8,128)S(1)}, f32[176,128]{1,0:T(8,128)S(1)}, u32[]{:S(2)}, u32[]{:S(2)}) collective-permute-start(f32[176,128]{1,0:T(8,128)S(1)} %get-tuple-element.23), channel_id=1, source_target_pairs={{1,0},{2,1},{3,2},{5,4},{6,5},{7,6},{9,8},{10,9},{11,10},{13,12},{... | collective-permute-start | bytes 270344 | tf_op jit(solution)/shard_map/ppermute | solution.py:480
  16.7 11.0 %collective-permute-start.2 = (f32[992,128]{1,0:T(8,128)S(1)}, f32[992,128]{1,0:T(8,128)S(1)}, u32[]{:S(2)}, u32[]{:S(2)}) collective-permute-start(f32[992,128]{1,0:T(8,128)S(1)} %get-tuple-element.28), channel_id=1, source_target_pairs={{0,4},{4,8},{8,12},{12,16},{16,20},{20,24},{24,28},{28,32},{32,36}... | collective-permute-start | bytes 1523720 | tf_op jit(solution)/shard_map/ppermute | solution.py:489
  21.8 10.3 %collective-permute-start.3 = (f32[992,128]{1,0:T(8,128)S(1)}, f32[992,128]{1,0:T(8,128)S(1)}, u32[]{:S(2)}, u32[]{:S(2)}) collective-permute-start(f32[992,128]{1,0:T(8,128)S(1)} %get-tuple-element.29), channel_id=1, source_target_pairs={{4,0},{8,4},{12,8},{16,12},{20,16},{24,20},{28,24},{32,28},{36,32}... | collective-permute-start | bytes 1523720 | tf_op jit(solution)/shard_map/ppermute | solution.py:488
  45.1 1.3 %collective-permute-start.4 = (f32[40,128]{1,0:T(8,128)S(1)}, f32[40,128]{1,0:T(8,128)S(1)}, u32[]{:S(2)}, u32[]{:S(2)}) collective-permute-start(f32[40,128]{1,0:T(8,128)S(1)} %get-tuple-element.30), channel_id=1, source_target_pairs={{0,4},{4,0},{1,5},{5,1},{2,6},{6,2},{3,7},{7,3},{8,12},{12,8},{9,1... | collective-permute-start | bytes 61448 | tf_op jit(solution)/shard_map/ppermute | solution.py:510

commit v4 on v3

--- a/solution.py
+++ b/solution.py
@@ -48,8 +48,35 @@
     return tuple(pltpu.with_memory_space_constraint(v, pltpu.VMEM) for v in values)
 
 
-def prepare_body(dom, sub_axis, rows_total, cols_total, source, initial, mass, slots, stiffness,
-                 ini_x, src_x, w_main, w_strip, to_left, to_right, acc):
+def distant(*values):
+    if INTERPRET:
+        return values
+    return tuple(pltpu.with_memory_space_constraint(v, pltpu.HBM) for v in values)
+
+
+MAIN_I = 0
+MAIN_S = 10 * 32
+MAIN_W = MAIN_S + 8 * 32
+MAIN_END = MAIN_W + NH * 16
+STRIP_I = 0
+STRIP_S = 10 * 8
+STRIP_W = STRIP_S + 8 * 8
+STRIP_END = STRIP_W + 4 * 16
+
+
+def prepare_body(dom, sub_axis, rows_total, cols_total, source_far, initial_far, mass_far, slots_far, stiffness_far,
+                 ini_m, src_m, ini_h, src_h, w_main, w_strip, to_left, to_right, to_up, to_down,
+                 acc, source, initial, mass, slots, stiffness, arrived):
+    copies = [
+        pltpu.make_async_copy(far_ref, near_ref, arrived.at[i])
+        for i, (far_ref, near_ref) in enumerate((
+            (slots_far, slots), (stiffness_far, stiffness), (mass_far, mass), (initial_far, initial),
+            (source_far, source)))
+    ]
+    for copy in copies:
+        copy.start()
+    for copy in copies[:3]:
+        copy.wait()
     row = lax.broadcasted_iota(jnp.int32, (NR, NC), 0) + lax.axis_index(dom) * NR
     col = lanes((NR, NC)) + lax.axis_index(sub_axis) * NC
     top, bottom = row == 0, row == rows_total - 1
@@ -90,6 +117,8 @@
         over_west = jnp.where(lane == NC - 1, west_turn, 0.0)
         main = acc[1, d] + (east_turn - over_east) + (west_turn - over_west)
         w_main[d] = main
+        to_up[MAIN_W + 16 * d:MAIN_W + 16 * d + 16, :] = main[0:16]
+        to_down[MAIN_W + 16 * d:MAIN_W + 16 * d + 16, :] = main[8:24]
         own = turn(jnp.where(lane < 4, main, 0.0) + over_west, 28)
         own = own + turn(jnp.where(lane >= 124, main, 0.0) + over_east, 4)
         strips[d // 4] = strips[d // 4] + turn(own, 32 * (d % 4))
@@ -102,6 +131,8 @@
         to_right[128 + 24 * j:152 + 24 * j, :] = pack_right[j]
         to_left[128 + 24 * j:152 + 24 * j, :] = pack_left[j]
 
+    for copy in copies[3:]:
+        copy.wait()
     lane = lanes((8, NC))
     place = lane % 32
     segment = lane // 32
@@ -114,8 +145,17 @@
             here = segment == g
             ini = initial[pl.ds(g * 128 + r, 8, stride=NR), :]
             src = source[pl.ds(g * 128 + r, 8, stride=NR), :]
-            ini_x[r, 8 * g:8 * g + 8, :] = ini
-            src_x[r, 8 * g:8 * g + 8, :] = src
+            at = 8 * g
+            ini_m[r, at:at + 8, :] = ini
+            src_m[r, at:at + 8, :] = src
+            if r < 10:
+                to_up[MAIN_I + 32 * r + at:MAIN_I + 32 * r + at + 8, :] = ini
+            if r >= 6:
+                to_down[MAIN_I + 32 * (r - 6) + at:MAIN_I + 32 * (r - 6) + at + 8, :] = ini
+            if r < 8:
+                to_up[MAIN_S + 32 * r + at:MAIN_S + 32 * r + at + 8, :] = src
+            else:
+                to_down[MAIN_S + 32 * (r - 8) + at:MAIN_S + 32 * (r - 8) + at + 8, :] = src
             turned = turn(ini, 4 + 32 * g)
             strip_i = jnp.where(here & (place < 4), turned, strip_i)
             left = jnp.where(here & (place >= 4) & (place < 14), turned, left)
@@ -128,83 +168,83 @@
             strip_s = jnp.where(here & (place >= 28), turned, strip_s)
             right = jnp.where(here & (place >= 18) & (place < 28), turned, right)
             right = jnp.where(here & (place >= 2) & (place < 12), turn(ini, 12 + 32 * g), right)
-        ini_x[r, 32:40, :] = strip_i
-        src_x[r, 32:40, :] = strip_s
+        ini_h[r] = strip_i
+        src_h[r] = strip_s
         to_right[8 * r:8 * r + 8, :] = right
         to_left[8 * r:8 * r + 8, :] = left
 
 
-ROW_I = 0
-ROW_S = 10 * 40
-ROW_W = ROW_S + 8 * 40
-ROW_H = ROW_W + NH * 16
-ROW_END = ROW_H + 4 * 16
-
-
-def columns_body(ini_x, src_x, w_main, w_strip, from_left, from_right,
-                 ini_o, src_o, main_o, strip_o, to_up, to_down):
+def columns_body(sub_axis, sub_count, ini_h, src_h, w_strip, from_left, from_right, ini_o, src_o, strip_o, to_up, to_down):
     lane = lanes((8, NC))
     place = lane % 32
     is_left = (place >= 18) & (place < 28)
     is_right = (place >= 4) & (place < 14)
+    at = lax.axis_index(sub_axis)
+    has_left, has_right = at > 0, at < sub_count - 1
     for r in range(NR):
-        left = from_left[8 * r:8 * r + 8, :]
-        right = from_right[8 * r:8 * r + 8, :]
-        ini_o[r, 0:32, :] = ini_x[r, 0:32, :]
-        src_o[r, 0:32, :] = src_x[r, 0:32, :]
-        ini_o[r, 32:40, :] = jnp.where(is_left, turn(left, 16), jnp.where(is_right, right, ini_x[r, 32:40, :]))
-        src_o[r, 32:40, :] = jnp.where(is_left, left, jnp.where(is_right, turn(right, -16), src_x[r, 32:40, :]))
+        left = jnp.where(has_left, from_left[8 * r:8 * r + 8, :], 0.0)
+        right = jnp.where(has_right, from_right[8 * r:8 * r + 8, :], 0.0)
+        ini = jnp.where(is_left, turn(left, 16), jnp.where(is_right, right, ini_h[r]))
+        src = jnp.where(is_left, left, jnp.where(is_right, turn(right, -16), src_h[r]))
+        ini_o[r] = ini
+        src_o[r] = src
+        if r < 10:
+            to_up[STRIP_I + 8 * r:STRIP_I + 8 * r + 8, :] = ini
+        if r >= 6:
+            to_down[STRIP_I + 8 * (r - 6):STRIP_I + 8 * (r - 6) + 8, :] = ini
+        if r < 8:
+            to_up[STRIP_S + 8 * r:STRIP_S + 8 * r + 8, :] = src
+        else:
+            to_down[STRIP_S + 8 * (r - 8):STRIP_S + 8 * (r - 8) + 8, :] = src
     lane = lanes((24, NC))
     strips = [w_strip[j] for j in range(4)]
     for d in range(NH):
         k = 16 * (d % 8)
         left = from_left[128 + 24 * (d // 8):152 + 24 * (d // 8), :]
         right = from_right[128 + 24 * (d // 8):152 + 24 * (d // 8), :]
-        left = jnp.where((lane >= 18) & (lane <= 28), turn(left, 16 - k), 0.0)
-        right = jnp.where((lane >= 3) & (lane <= 13), turn(right, -k), 0.0)
+        left = jnp.where((lane >= 18) & (lane <= 28) & has_left, turn(left, 16 - k), 0.0)
+        right = jnp.where((lane >= 3) & (lane <= 13) & has_right, turn(right, -k), 0.0)
         strips[d // 4] = strips[d // 4] + turn(left + right, 32 * (d % 4))
-        main = w_main[d]
-        main = main + jnp.where(lane == 0, turn(left, -28), 0.0)
-        main = main + jnp.where(lane == NC - 1, turn(right, 124), 0.0)
-        main_o[d] = main
-        to_up[ROW_W + 16 * d:ROW_W + 16 * d + 16, :] = main[0:16]
-        to_down[ROW_W + 16 * d:ROW_W + 16 * d + 16, :] = main[8:24]
     for j in range(4):
         strip_o[j] = strips[j]
-        to_up[ROW_H + 16 * j:ROW_H + 16 * j + 16, :] = strips[j][0:16]
-        to_down[ROW_H + 16 * j:ROW_H + 16 * j + 16, :] = strips[j][8:24]
-    for i in range(10):
-        to_up[ROW_I + 40 * i:ROW_I + 40 * i + 40, :] = ini_o[i]
-        to_down[ROW_I + 40 * i:ROW_I + 40 * i + 40, :] = ini_o[6 + i]
-    for i in range(8):
-        to_up[ROW_S + 40 * i:ROW_S + 40 * i + 40, :] = src_o[i]
-        to_down[ROW_S + 40 * i:ROW_S + 40 * i + 40, :] = src_o[8 + i]
-
-
-def basis_body(scale, ini_x, src_x, w_main, w_strip, from_up, from_down, basis, packed,
+        to_up[STRIP_W + 16 * j:STRIP_W + 16 * j + 16, :] = strips[j][0:16]
+        to_down[STRIP_W + 16 * j:STRIP_W + 16 * j + 16, :] = strips[j][8:24]
+
+
+def basis_body(dom, dom_count, scale, ini_m, src_m, ini_h, src_h, w_main, w_strip, up_main, down_main, up_strip, down_strip,
+               basis, packed,
                coef_m, coef_h, ini_v, src_v, vec_a, vec_b, sums):
     lane = lanes((8, NC))
     segment = lane // 32
     own = (1, 2, 3)
+    at = lax.axis_index(dom)
+    has_up, has_down = at > 0, at < dom_count - 1
+
+    def upper(ref, start, size=8):
+        return jnp.where(has_up, ref[start:start + size, :], 0.0)
+
+    def lower(ref, start, size=8):
+        return jnp.where(has_down, ref[start:start + size, :], 0.0)
+
     for d in range(NH):
         for t in range(5):
             main = None
             strip = None
             parts = []
             if t < 2:
-                parts.append((from_up[ROW_W + 16 * d + 8 * t:ROW_W + 16 * d + 8 * t + 8, :],
-                              from_up[ROW_H + 16 * (d // 4) + 8 * t:ROW_H + 16 * (d // 4) + 8 * t + 8, :]))
+                parts.append((upper(up_main, MAIN_W + 16 * d + 8 * t), upper(up_strip, STRIP_W + 16 * (d // 4) + 8 * t)))
             if t in own:
                 parts.append((w_main[d, 8 * t - 8:8 * t, :], w_strip[d // 4, 8 * t - 8:8 * t, :]))
             if t > 2:
                 s = 8 * (t - 3)
-                parts.append((from_down[ROW_W + 16 * d + s:ROW_W + 16 * d + s + 8, :],
-                              from_down[ROW_H + 16 * (d // 4) + s:ROW_H + 16 * (d // 4) + s + 8, :]))
+                parts.append((lower(down_main, MAIN_W + 16 * d + s), lower(down_strip, STRIP_W + 16 * (d // 4) + s)))
             main = sum(p[0] for p in parts[1:]) + parts[0][0] if len(parts) > 1 else parts[0][0]
             strip = sum(p[1] for p in parts[1:]) + parts[0][1] if len(parts) > 1 else parts[0][1]
             strip = jnp.where(segment == d % 4, strip, 0.0)
             strip = strip + turn(strip, 32)
             strip = strip + turn(strip, 64)
+            main = jnp.where(lane == 0, turn(strip, -28), main)
+            main = jnp.where(lane == NC - 1, turn(strip, 124), main)
             coef_m[d, 8 * t:8 * t + 8, :] = main
             coef_h[d, 8 * t:8 * t + 8, :] = strip
             dc = HALF[d][1]
@@ -219,14 +259,20 @@
                 coef_h[i, 8 * t:8 * t + 8, :] = turn(strip, dc)
 
     for i in range(10):
-        ini_v[i] = from_up[ROW_I + 40 * i:ROW_I + 40 * i + 40, :]
-        ini_v[26 + i] = from_down[ROW_I + 40 * i:ROW_I + 40 * i + 40, :]
+        ini_v[i, 0:32] = upper(up_main, MAIN_I + 32 * i, 32)
+        ini_v[i, 32:40] = upper(up_strip, STRIP_I + 8 * i)
+        ini_v[26 + i, 0:32] = lower(down_main, MAIN_I + 32 * i, 32)
+        ini_v[26 + i, 32:40] = lower(down_strip, STRIP_I + 8 * i)
     for i in range(8):
-        src_v[2 + i] = from_up[ROW_S + 40 * i:ROW_S + 40 * i + 40, :]
-        src_v[26 + i] = from_down[ROW_S + 40 * i:ROW_S + 40 * i + 40, :]
+        src_v[2 + i, 0:32] = upper(up_main, MAIN_S + 32 * i, 32)
+        src_v[2 + i, 32:40] = upper(up_strip, STRIP_S + 8 * i)
+        src_v[26 + i, 0:32] = lower(down_main, MAIN_S + 32 * i, 32)
+        src_v[26 + i, 32:40] = lower(down_strip, STRIP_S + 8 * i)
     for i in range(NR):
-        ini_v[10 + i] = ini_x[i]
-        src_v[10 + i] = src_x[i]
+        ini_v[10 + i, 0:32] = ini_m[i]
+        ini_v[10 + i, 32:40] = ini_h[i]
+        src_v[10 + i, 0:32] = src_m[i]
+        src_v[10 + i, 32:40] = src_h[i]
 
     place = lane % 32
     inner = jnp.where((place >= 30) | (place < 2), segment, 4)
@@ -460,8 +506,8 @@
     return far(*dims) if INTERPRET else pltpu.VMEM(dims, F32)
 
 
-def neighbours(count, step):
-    return [(i, i + step) for i in range(count) if 0 <= i + step < count]
+def ring(count, step):
+    return [(i, (i + step) % count) for i in range(count)]
 
 
 def on_device(dom, sub, dom_count, sub_count, reduce_groups, source, initial, lumped_mass, node_slots, stiffness):
@@ -470,26 +516,40 @@
     def prepare(*refs):
         prepare_body(dom, sub, rows_total, cols_total, *refs)
 
-    ini_x, src_x, w_main, w_strip, to_left, to_right = call(
+    ini_m, src_m, ini_h, src_h, w_main, w_strip, to_left, to_right, to_up, to_down = call(
         prepare,
-        (shape(NR, 40, NC), shape(NR, 40, NC), shape(NH, 24, NC), shape(4, 24, NC), shape(176, NC), shape(176, NC)),
-        scratch=[pltpu.VMEM((3, NH, 24, NC), F32)],
+        (shape(NR, NF, NC), shape(NR, NF, NC), shape(NR, 8, NC), shape(NR, 8, NC), shape(NH, 24, NC), shape(4, 24, NC),
+         shape(176, NC), shape(176, NC), shape(MAIN_END, NC), shape(MAIN_END, NC)),
+        scratch=[
+            pltpu.VMEM((3, NH, 24, NC), F32),
+            pltpu.VMEM((NF * NR, NC), F32),
+            pltpu.VMEM((NF * NR, NC), F32),
+            pltpu.VMEM((NR, NC), F32),
+            pltpu.VMEM((6, NR, NC), jnp.int32),
+            pltpu.VMEM((36, NR, NC), F32),
+            pltpu.SemaphoreType.DMA((5,)),
+        ],
+        in_specs=[pl.BlockSpec(memory_space=pl.ANY)] * 5,
         name="prepare",
-    )(source.reshape(NF * NR, NC), initial.reshape(NF * NR, NC), lumped_mass, node_slots,
-      stiffness.reshape(36, NR, NC))
-    from_right = lax.ppermute(to_left, sub, neighbours(sub_count, -1))
-    from_left = lax.ppermute(to_right, sub, neighbours(sub_count, 1))
-    ini_x, src_x, w_main, w_strip, to_up, to_down = call(
-        columns_body,
-        (shape(NR, 40, NC), shape(NR, 40, NC), shape(NH, 24, NC), shape(4, 24, NC), shape(ROW_END, NC),
-         shape(ROW_END, NC)),
+    )(*distant(source.reshape(NF * NR, NC), initial.reshape(NF * NR, NC), lumped_mass, node_slots,
+               stiffness.reshape(36, NR, NC)))
+    from_right = lax.ppermute(to_left, sub, ring(sub_count, -1))
+    from_left = lax.ppermute(to_right, sub, ring(sub_count, 1))
+    down_main = lax.ppermute(to_up, dom, ring(dom_count, -1))
+    up_main = lax.ppermute(to_down, dom, ring(dom_count, 1))
+    def columns(*refs):
+        columns_body(sub, sub_count, *refs)
+
+    ini_h, src_h, w_strip, to_up, to_down = call(
+        columns,
+        (shape(NR, 8, NC), shape(NR, 8, NC), shape(4, 24, NC), shape(STRIP_END, NC), shape(STRIP_END, NC)),
         name="columns",
-    )(*near(ini_x, src_x, w_main, w_strip, from_left, from_right))
-    from_down = lax.ppermute(to_up, dom, neighbours(dom_count, -1))
-    from_up = lax.ppermute(to_down, dom, neighbours(dom_count, 1))
+    )(*near(ini_h, src_h, w_strip, from_left, from_right))
+    down_strip = lax.ppermute(to_up, dom, ring(dom_count, -1))
+    up_strip = lax.ppermute(to_down, dom, ring(dom_count, 1))
 
     def products(*refs):
-        basis_body(1.0 / float(rows_total * cols_total), *refs)
+        basis_body(dom, dom_count, 1.0 / float(rows_total * cols_total), *refs)
 
     basis, packed = call(
         products,
@@ -504,7 +564,7 @@
             pltpu.VMEM((96, NC), F32),
         ],
         name="products",
-    )(*near(ini_x, src_x, w_main, w_strip, from_up, from_down))
+    )(*near(ini_m, src_m, ini_h, src_h, w_main, w_strip, up_main, down_main, up_strip, down_strip))
     for i, (axes, count) in enumerate(reduce_groups):
         if count == 2:
             gathered = jnp.stack([packed, lax.ppermute(packed, axes, [(0, 1), (1, 0)])])

time: 86.8 us -> 77.3 us (0.89)
  waiting for transfers between devices: 13.5 us -> 3.72 us
  starting transfers between devices: 12.4 us -> 20 us
  blocking collectives: 32.8 us -> 28.4 us
  local copies, waits for them, and re-layouts: 4.39 us -> 0.04 us
  Pallas kernels: 21.9 us -> 23.7 us
    ppermute x4 -> x6, waiting for transfers between devices: 12.4 us -> 2.87 us  [the longest x1 1.91 us: on_device(): from_left = lax.ppermute(to_right, sub, ring(sub_count, 1))]
    ppermute x1, starting transfers between devices: 0.09 us -> 6.5 us  [on_device(): gathered = jnp.stack([packed, lax.ppermute(packed, axes, [(0, 1), (1, 0)])])]
    all_to_all x2, blocking collectives: 32.8 us -> 28.4 us  [on_device(): lax.all_to_all(jnp.broadcast_to(packed[None], (count, 40, NC)), axes, 0, 0)]
    unnamed x10 -> x0, local copies, waits for them, and re-layouts: 4.35 us -> none
    pallas_call x1, Pallas kernels: 12.9 us -> 14.4 us  [on_device(): call(products, (shape(NR, 160, NC), shape(40, NC)), scratch=[pltpu.VMEM((...]
    ppermute x4 -> x6, starting transfers between devices: 12.3 us -> 13.5 us  [the longest x1 4.83 us: on_device(): down_strip = lax.ppermute(to_up, dom, ring(dom_count, -1))]
  transfers between devices with their start and end apart: 5 -> 7, of which waited for: 5 -> 4; matrix products, arithmetic and copies ran while one was open for 0% -> 0% of each run, Pallas kernels for 0% -> 0%
where the time goes in v4:
time: 77.3 us; the launch traced here: 76.6 us
  blocking collectives  28.4 us (37%)
  Pallas kernels  23.7 us (31%)
  starting transfers between devices  20 us (26%)
  waiting for transfers between devices  3.72 us (5%)
    all_to_all x2, blocking collectives, on_device(): lax.all_to_all(jnp.broadcast_to(packed[None], (count, 40, NC)), axes, 0, 0)  28.4 us
    pallas_call x1, Pallas kernels, on_device(): call(products, (shape(NR, 160, NC), shape(40, NC)), scratch=[pltpu.VMEM((...  14.4 us
    pallas_call x1, Pallas kernels, on_device(): call(solve_body, (far(NF * NR, NC), far(128, 128)), scratch=[pltpu.VMEM((...  6.52 us
    ppermute x1, starting transfers between devices, on_device(): gathered = jnp.stack([packed, lax.ppermute(packed, axes, [(0, 1), (1, 0)])])  6.5 us
    ppermute x1, starting transfers between devices, on_device(): down_strip = lax.ppermute(to_up, dom, ring(dom_count, -1))  4.83 us
    ppermute x1, starting transfers between devices, on_device(): up_main = lax.ppermute(to_down, dom, ring(dom_count, 1))  2.67 us
    ppermute x1, starting transfers between devices, on_device(): up_strip = lax.ppermute(to_down, dom, ring(dom_count, 1))  2.63 us
    pallas_call x1, Pallas kernels, on_device(): call(prepare, (shape(NR, NF, NC), shape(NR, NF, NC), shape(NR, 8, NC), sh...  2.47 us
  transfers between devices with their start and end apart: 7, of which 4 were waited for; matrix products, arithmetic and copies ran while one was open for 0% of the time, Pallas kernels for 0%

profile of v4, /device:TPU:1, one launch (start us, length us, event | category | flops | bytes accessed | tf_op | source)
XLA Modules:
  0.0 76.6 jit_solution(4101668298039646297)
XLA Ops:
  0.6 2.5 %prepare.1 = (f32[16,32,128]{2,1,0:T(8,128)S(1)}, f32[16,32,128]{2,1,0:T(8,128)S(1)}, f32[16,8,128]{2,1,0:T(8,128)S(1)}, f32[16,8,128]{2,1,0:T(8,128)S(1)}, f32[...) custom-call(f32[512,128]{1,0:T(8,128)} %bitcast.5, ...), custom_call_target="tpu_custom_call" | custom-call | tf_op jit(solution)/shard_map/prepare/pallas_call | solution.py:519
  3.1 2.7 %collective-permute-start.2 = (f32[784,128]{1,0:T(8,128)S(1)}, f32[784,128]{1,0:T(8,128)S(1)}, u32[]{:S(2)}, u32[]{:S(2)}) collective-permute-start(f32[784,128]{1,0:T(8,128)S(1)} %get-tuple-element.32), channel_id=1, source_target_pairs={{0,4},{4,8},{8,12},{12,16},{16,20},{20,24},{24,28},{28,32},{32,36}... | collective-permute-start | bytes 1204232 | tf_op jit(solution)/shard_map/ppermute | solution.py:539
  5.8 0.7 collective-permute-start.3
  6.5 0.6 collective-permute-start
  7.1 2.1 %collective-permute-start.1 = (f32[176,128]{1,0:T(8,128)S(1)}, f32[176,128]{1,0:T(8,128)S(1)}, u32[]{:S(2)}, u32[]{:S(2)}) collective-permute-start(f32[176,128]{1,0:T(8,128)S(1)} %get-tuple-element.27), channel_id=1, source_target_pairs={{0,3},{1,0},{2,1},{3,2},{4,7},{5,4},{6,5},{7,6},{8,11},{9,8},{10,9... | collective-permute-start | bytes 270344 | tf_op jit(solution)/shard_map/ppermute | solution.py:536
  9.2 1.9 %collective-permute-done.refs_3_ = f32[176,128]{1,0:T(8,128)S(1)} collective-permute-done((f32[176,128]{1,0:T(8,128)S(1)}, f32[176,128]{1,0:T(8,128)S(1)}, u32[]{:S(2)}, u32[]{:S(2)}) %collective-permute-start) | collective-permute-done | bytes 90144 | tf_op jit(solution)/shard_map/ppermute | solution.py:537
  11.1 0.0 collective-permute-done.1.refs_4_
  11.1 0.3 columns.1
  11.3 2.6 %collective-permute-start.4 = (f32[208,128]{1,0:T(8,128)S(1)}, f32[208,128]{1,0:T(8,128)S(1)}, u32[]{:S(2)}, u32[]{:S(2)}) collective-permute-start(f32[208,128]{1,0:T(8,128)S(1)} %get-tuple-element.34), channel_id=1, source_target_pairs={{0,4},{4,8},{8,12},{12,16},{16,20},{20,24},{24,28},{28,32},{32,36}... | collective-permute-start | bytes 319496 | tf_op jit(solution)/shard_map/ppermute | solution.py:549
  14.0 4.8 %collective-permute-start.5 = (f32[208,128]{1,0:T(8,128)S(1)}, f32[208,128]{1,0:T(8,128)S(1)}, u32[]{:S(2)}, u32[]{:S(2)}) collective-permute-start(f32[208,128]{1,0:T(8,128)S(1)} %get-tuple-element.35), channel_id=1, source_target_pairs={{0,252},{4,0},{8,4},{12,8},{16,12},{20,16},{24,20},{28,24},{32,28}... | collective-permute-start | bytes 319496 | tf_op jit(solution)/shard_map/ppermute | solution.py:548
  18.8 0.7 collective-permute-done.4.refs_8_
  19.5 0.2 collective-permute-done.5.refs_9_
  19.8 0.0 collective-permute-done.2.refs_6_
  19.8 0.0 collective-permute-done.3.refs_7_
  19.8 14.4 %products.1 = (f32[16,160,128]{2,1,0:T(8,128)S(1)}, f32[40,128]{1,0:T(8,128)S(1)}) custom-call(f32[16,32,128]{2,1,0:T(8,128)S(1)} %get-tuple-element.21.refs_0_, f32[16,32,128]{2,1,0:T(8,128)S(1)} %get-tuple-element.22.refs_1_, f32[16,8,128]{2,1,0:T(8,128)S(1)} %get-tuple-element.28.refs_2_, f32[16,8,128]{2,1,0:T(8,128)S(1)} %get-tuple-element.29.refs_3_, ...), custom_call_target="tpu_custom_call" | custom-call | tf_op jit(solution)/shard_map/products/pallas_call | solution.py:554
  34.2 6.5 %collective-permute-start.6 = (f32[40,128]{1,0:T(8,128)S(1)}, f32[40,128]{1,0:T(8,128)S(1)}, u32[]{:S(2)}, u32[]{:S(2)}) collective-permute-start(f32[40,128]{1,0:T(8,128)S(1)} %get-tuple-element.36), channel_id=1, source_target_pairs={{0,4},{4,0},{1,5},{5,1},{2,6},{6,2},{3,7},{7,3},{8,12},{12,8},{9,1... | collective-permute-start | bytes 61448 | tf_op jit(solution)/shard_map/ppermute | solution.py:570
  40.7 0.8 %collective-permute-done.6 = f32[40,128]{1,0:T(8,128)S(1)} collective-permute-done((f32[40,128]{1,0:T(8,128)S(1)}, f32[40,128]{1,0:T(8,128)S(1)}, u32[]{:S(2)}, u32[]{:S(2)}) %collective-permute-start.6) | collective-permute-done | bytes 20512 | tf_op jit(solution)/shard_map/ppermute | solution.py:570
  41.6 11.8 %all_to_all.10 = f32[16,40,128]{2,1,0:T(8,128)S(1)} all-to-all(f32[16,40,128]{2,1,0:T(8,128)S(1)} %broadcast_in_dim.4), channel_id=1, replica_groups=mesh['z'=8,'x'=4,'c'=2,'sub'=4] {'x','sub'}, dimensions={0} | all-to-all | bytes 655360 | tf_op jit(solution)/shard_map/all_to_all | solution.py:572
  53.4 16.7 %all_to_all.11.parts = f32[8,40,128]{2,1,0:T(8,128)S(1)} all-to-all(f32[8,40,128]{2,1,0:T(8,128)S(1)} %broadcast_in_dim.5), channel_id=1, replica_groups=mesh['z'=8,'x'=4,'c'=2,'sub'=4] {'z'}, dimensions={0} | all-to-all | bytes 327680 | tf_op jit(solution)/shard_map/all_to_all | solution.py:572
  70.0 6.5 %solve.1 = (f32[512,128]{1,0:T(8,128)}, f32[128,128]{1,0:T(8,128)}) custom-call(f32[8,40,128]{2,1,0:T(8,128)S(1)} %all_to_all.11.parts, f32[16,160,128]{2,1,0:T(8,128)S(1)} %get-tuple-element.37.basis), custom_call_target="tpu_custom_call" | custom-call | tf_op jit(solution)/shard_map/solve/pallas_call | solution.py:575
  (4 shorter events, 0.1 us)
Async XLA Ops:
  3.1 16.7 %collective-permute-start.2 = (f32[784,128]{1,0:T(8,128)S(1)}, f32[784,128]{1,0:T(8,128)S(1)}, u32[]{:S(2)}, u32[]{:S(2)}) collective-permute-start(f32[784,128]{1,0:T(8,128)S(1)} %get-tuple-element.32), channel_id=1, source_target_pairs={{0,4},{4,8},{8,12},{12,16},{16,20},{20,24},{24,28},{28,32},{32,36}... | collective-permute-start | bytes 1204232 | tf_op jit(solution)/shard_map/ppermute | solution.py:539
  5.8 14.0 %collective-permute-start.3 = (f32[784,128]{1,0:T(8,128)S(1)}, f32[784,128]{1,0:T(8,128)S(1)}, u32[]{:S(2)}, u32[]{:S(2)}) collective-permute-start(f32[784,128]{1,0:T(8,128)S(1)} %get-tuple-element.33), channel_id=1, source_target_pairs={{0,252},{4,0},{8,4},{12,8},{16,12},{20,16},{24,20},{28,24},{32,28}... | collective-permute-start | bytes 1204232 | tf_op jit(solution)/shard_map/ppermute | solution.py:538
  6.5 4.6 %collective-permute-start = (f32[176,128]{1,0:T(8,128)S(1)}, f32[176,128]{1,0:T(8,128)S(1)}, u32[]{:S(2)}, u32[]{:S(2)}) collective-permute-start(f32[176,128]{1,0:T(8,128)S(1)} %get-tuple-element.26), channel_id=1, source_target_pairs={{0,1},{1,2},{2,3},{3,0},{4,5},{5,6},{6,7},{7,4},{8,9},{9,10},{10,1... | collective-permute-start | bytes 270344 | tf_op jit(solution)/shard_map/ppermute | solution.py:537
  7.1 4.0 %collective-permute-start.1 = (f32[176,128]{1,0:T(8,128)S(1)}, f32[176,128]{1,0:T(8,128)S(1)}, u32[]{:S(2)}, u32[]{:S(2)}) collective-permute-start(f32[176,128]{1,0:T(8,128)S(1)} %get-tuple-element.27), channel_id=1, source_target_pairs={{0,3},{1,0},{2,1},{3,2},{4,7},{5,4},{6,5},{7,6},{8,11},{9,8},{10,9... | collective-permute-start | bytes 270344 | tf_op jit(solution)/shard_map/ppermute | solution.py:536
  11.3 8.2 %collective-permute-start.4 = (f32[208,128]{1,0:T(8,128)S(1)}, f32[208,128]{1,0:T(8,128)S(1)}, u32[]{:S(2)}, u32[]{:S(2)}) collective-permute-start(f32[208,128]{1,0:T(8,128)S(1)} %get-tuple-element.34), channel_id=1, source_target_pairs={{0,4},{4,8},{8,12},{12,16},{16,20},{20,24},{24,28},{28,32},{32,36}... | collective-permute-start | bytes 319496 | tf_op jit(solution)/shard_map/ppermute | solution.py:549
  14.0 5.8 %collective-permute-start.5 = (f32[208,128]{1,0:T(8,128)S(1)}, f32[208,128]{1,0:T(8,128)S(1)}, u32[]{:S(2)}, u32[]{:S(2)}) collective-permute-start(f32[208,128]{1,0:T(8,128)S(1)} %get-tuple-element.35), channel_id=1, source_target_pairs={{0,252},{4,0},{8,4},{12,8},{16,12},{20,16},{24,20},{28,24},{32,28}... | collective-permute-start | bytes 319496 | tf_op jit(solution)/shard_map/ppermute | solution.py:548
  34.2 7.3 %collective-permute-start.6 = (f32[40,128]{1,0:T(8,128)S(1)}, f32[40,128]{1,0:T(8,128)S(1)}, u32[]{:S(2)}, u32[]{:S(2)}) collective-permute-start(f32[40,128]{1,0:T(8,128)S(1)} %get-tuple-element.36), channel_id=1, source_target_pairs={{0,4},{4,0},{1,5},{5,1},{2,6},{6,2},{3,7},{7,3},{8,12},{12,8},{9,1... | collective-permute-start | bytes 61448 | tf_op jit(solution)/shard_map/ppermute | solution.py:570

commit v5 on v4

--- a/solution.py
+++ b/solution.py
@@ -1,16 +1,15 @@
 import jax
 import jax.numpy as jnp
-import numpy as np
 from jax import lax
 from jax.experimental import pallas as pl
 from jax.experimental.pallas import tpu as pltpu
 from jax.sharding import Mesh, PartitionSpec as P
 
+
 STEPS = 4
 NF = 32
 NR = 16
 NC = 128
-HALO = 10
 INTERPRET = False
 F32 = jnp.float32
 
@@ -275,10 +274,21 @@
         src_v[10 + i, 32:40] = src_h[i]
 
     place = lane % 32
-    inner = jnp.where((place >= 30) | (place < 2), segment, 4)
+    edge = (lane < 2) | (lane >= NC - 2)
+    from_low = place < 2
     tail = place >= 30
-    head = lane < 2
-    foot = lane >= NC - 2
+    second = (lane >= 16) & (lane < 48)
+    upper_pair = (lane >= 48) & (lane < 112)
+
+    def edges_of(strip):
+        both = jnp.where(from_low, turn(strip, -28), turn(strip, -4))
+        return [turn(both, -32 * g) for g in range(4)]
+
+    def inner_of(mains, strip):
+        low = jnp.where(second, turn(mains[1], 32), mains[0])
+        high = jnp.where(second, turn(mains[3], 32), mains[2])
+        both = jnp.where(upper_pair, turn(high, 64), low)
+        return jnp.where(tail, turn(both, 28), jnp.where(from_low, turn(both, 4), strip))
 
     def image(vec, r):
         def spread(ref):
@@ -305,18 +315,20 @@
                 parts.append(turn(part, -dc))
             return ((parts[0] + parts[1]) + (parts[2] + parts[3])) + parts[4]
 
-        coef_strip = spread(coef_h)
-        strip = unit(coef_strip, 4)
+        strip = unit(spread(coef_h), 4)
         coef = spread(coef_m)
-        fixed = strip
-        result = []
-        for g in range(4):
-            main = unit(coef, g)
-            edge = jnp.where(tail, turn(main, 32 * g + 28), turn(main, 32 * g + 4))
-            fixed = jnp.where(inner == g, edge, fixed)
-            out = jnp.where(head, turn(strip, 100 - 32 * g), main)
-            result.append(jnp.where(foot, turn(strip, 124 - 32 * g), out))
-        return result + [fixed]
+        edges = edges_of(strip)
+        result = [jnp.where(edge, edges[g], unit(coef, g)) for g in range(4)]
+        return result + [strip]
+
+    def mended(vec, r):
+        mains = [vec[r + 10, 8 * g:8 * g + 8, :] for g in range(4)]
+        return inner_of(mains, vec[r + 10, 32:40, :])
+
+    def mend(vec, rows):
+        strips = [mended(vec, r) for r in rows]
+        for r, strip in zip(rows, strips):
+            vec[r + 10, 32:40, :] = strip
 
     vectors = (vec_a, vec_b)
     for step in range(-1, STEPS):
@@ -324,17 +336,21 @@
         source_vec = ini_v if step < 0 else vectors[step % 2]
         target_vec = vec_a if step < 0 else vectors[(step + 1) % 2]
 
-        def some_rows(rows, inside, step=step, source_vec=source_vec, target_vec=target_vec):
+        def some_rows(rows, before, inside, step=step, source_vec=source_vec, target_vec=target_vec):
+            more = step + 1 < STEPS
+            strips = [mended(target_vec, r) for r in before] if more else []
             values = []
             for r in rows:
                 units = image(source_vec, r)
                 olds = src_v if step < 0 else source_vec
                 nexts = []
-                if step + 1 < STEPS:
+                if more:
                     for u in range(5):
                         old = olds[r + 10, 8 * u:8 * u + 8, :]
                         nexts.append(old - units[u] if step < 0 else units[u] - 2.0 * old)
                 values.append((r, units, nexts))
+            for r, strip in zip(before, strips):
+                target_vec[r + 10, 32:40, :] = strip
             for r, units, nexts in values:
                 for u, value in enumerate(nexts):
                     target_vec[r + 10, 8 * u:8 * u + 8, :] = value
@@ -344,19 +360,27 @@
                         at = 32 + 32 * step + 8 * u
                         basis[r, at:at + 8, :] = kept[u]
 
-        def outer(i, carry, reach=reach, some_rows=some_rows):
-            top = 2 * i - reach
-            bottom = NR + 2 * i
-            some_rows((top, top + 1, bottom, bottom + 1), False)
+        def outer_rows(i, reach=reach):
+            return (2 * i - reach, 2 * i - reach + 1, NR + 2 * i, NR + 2 * i + 1)
+
+        def middle_rows(i):
+            return tuple(4 * i + j for j in range(4))
+
+        def outer(i, carry, some_rows=some_rows, outer_rows=outer_rows):
+            some_rows(outer_rows(i), outer_rows(jnp.maximum(i - 1, 0)), False)
             return carry
 
         def middle(i, carry, some_rows=some_rows):
-            some_rows(tuple(4 * i + j for j in range(4)), True)
+            some_rows(middle_rows(i), middle_rows(jnp.maximum(i - 1, 0)), True)
             return carry
 
+        last = middle_rows(NR // 4 - 1)
         if reach > 0:
             lax.fori_loop(0, reach // 2, outer, 0)
+            last = last + outer_rows(reach // 2 - 1)
         lax.fori_loop(0, NR // 4, middle, 0)
+        if step + 1 < STEPS:
+            mend(target_vec, last)
 
     sums[...] = jnp.zeros(sums.shape, F32)
 
@@ -537,6 +561,7 @@
     from_left = lax.ppermute(to_right, sub, ring(sub_count, 1))
     down_main = lax.ppermute(to_up, dom, ring(dom_count, -1))
     up_main = lax.ppermute(to_down, dom, ring(dom_count, 1))
+
     def columns(*refs):
         columns_body(sub, sub_count, *refs)
 

time: 77.3 us -> 76.3 us (0.987)
  Pallas kernels: 23.7 us -> 22.7 us
    pallas_call x1, Pallas kernels: 14.4 us -> 13.4 us  [on_device(): call(products, (shape(NR, 160, NC), shape(40, NC)), scratch=[pltpu.VMEM((...]
where the time goes in v5:
time: 76.3 us; the launch traced here: 75.5 us
  blocking collectives  28.4 us (37%)
  Pallas kernels  22.7 us (30%)
  starting transfers between devices  20 us (26%)
  waiting for transfers between devices  3.72 us (5%)
    all_to_all x2, blocking collectives, on_device(): lax.all_to_all(jnp.broadcast_to(packed[None], (count, 40, NC)), axes, 0, 0)  28.4 us
    pallas_call x1, Pallas kernels, on_device(): call(products, (shape(NR, 160, NC), shape(40, NC)), scratch=[pltpu.VMEM((...  13.4 us
    pallas_call x1, Pallas kernels, on_device(): call(solve_body, (far(NF * NR, NC), far(128, 128)), scratch=[pltpu.VMEM((...  6.52 us
    ppermute x1, starting transfers between devices, on_device(): gathered = jnp.stack([packed, lax.ppermute(packed, axes, [(0, 1), (1, 0)])])  6.5 us
    ppermute x1, starting transfers between devices, on_device(): down_strip = lax.ppermute(to_up, dom, ring(dom_count, -1))  4.83 us
    ppermute x1, starting transfers between devices, on_device(): up_main = lax.ppermute(to_down, dom, ring(dom_count, 1))  2.67 us
    ppermute x1, starting transfers between devices, on_device(): up_strip = lax.ppermute(to_down, dom, ring(dom_count, 1))  2.63 us
    pallas_call x1, Pallas kernels, on_device(): call(prepare, (shape(NR, NF, NC), shape(NR, NF, NC), shape(NR, 8, NC), sh...  2.47 us
  transfers between devices with their start and end apart: 7, of which 4 were waited for; matrix products, arithmetic and copies ran while one was open for 0% of the time, Pallas kernels for 0%

profile of v5, /device:TPU:1, one launch (start us, length us, event | category | flops | bytes accessed | tf_op | source)
XLA Modules:
  0.0 75.5 jit_solution(2574535157928495744)
XLA Ops:
  0.6 2.5 %prepare.1 = (f32[16,32,128]{2,1,0:T(8,128)S(1)}, f32[16,32,128]{2,1,0:T(8,128)S(1)}, f32[16,8,128]{2,1,0:T(8,128)S(1)}, f32[16,8,128]{2,1,0:T(8,128)S(1)}, f32[...) custom-call(f32[512,128]{1,0:T(8,128)} %bitcast.5, ...), custom_call_target="tpu_custom_call" | custom-call | tf_op jit(solution)/shard_map/prepare/pallas_call | solution.py:543
  3.1 2.7 %collective-permute-start.2 = (f32[784,128]{1,0:T(8,128)S(1)}, f32[784,128]{1,0:T(8,128)S(1)}, u32[]{:S(2)}, u32[]{:S(2)}) collective-permute-start(f32[784,128]{1,0:T(8,128)S(1)} %get-tuple-element.32), channel_id=1, source_target_pairs={{0,4},{4,8},{8,12},{12,16},{16,20},{20,24},{24,28},{28,32},{32,36}... | collective-permute-start | bytes 1204232 | tf_op jit(solution)/shard_map/ppermute | solution.py:563
  5.8 0.7 collective-permute-start.3
  6.5 0.6 collective-permute-start
  7.1 2.1 %collective-permute-start.1 = (f32[176,128]{1,0:T(8,128)S(1)}, f32[176,128]{1,0:T(8,128)S(1)}, u32[]{:S(2)}, u32[]{:S(2)}) collective-permute-start(f32[176,128]{1,0:T(8,128)S(1)} %get-tuple-element.27), channel_id=1, source_target_pairs={{0,3},{1,0},{2,1},{3,2},{4,7},{5,4},{6,5},{7,6},{8,11},{9,8},{10,9... | collective-permute-start | bytes 270344 | tf_op jit(solution)/shard_map/ppermute | solution.py:560
  9.2 1.9 %collective-permute-done.refs_3_ = f32[176,128]{1,0:T(8,128)S(1)} collective-permute-done((f32[176,128]{1,0:T(8,128)S(1)}, f32[176,128]{1,0:T(8,128)S(1)}, u32[]{:S(2)}, u32[]{:S(2)}) %collective-permute-start) | collective-permute-done | bytes 90144 | tf_op jit(solution)/shard_map/ppermute | solution.py:561
  11.1 0.0 collective-permute-done.1.refs_4_
  11.1 0.3 columns.1
  11.3 2.6 %collective-permute-start.4 = (f32[208,128]{1,0:T(8,128)S(1)}, f32[208,128]{1,0:T(8,128)S(1)}, u32[]{:S(2)}, u32[]{:S(2)}) collective-permute-start(f32[208,128]{1,0:T(8,128)S(1)} %get-tuple-element.34), channel_id=1, source_target_pairs={{0,4},{4,8},{8,12},{12,16},{16,20},{20,24},{24,28},{28,32},{32,36}... | collective-permute-start | bytes 319496 | tf_op jit(solution)/shard_map/ppermute | solution.py:574
  14.0 4.8 %collective-permute-start.5 = (f32[208,128]{1,0:T(8,128)S(1)}, f32[208,128]{1,0:T(8,128)S(1)}, u32[]{:S(2)}, u32[]{:S(2)}) collective-permute-start(f32[208,128]{1,0:T(8,128)S(1)} %get-tuple-element.35), channel_id=1, source_target_pairs={{0,252},{4,0},{8,4},{12,8},{16,12},{20,16},{24,20},{28,24},{32,28}... | collective-permute-start | bytes 319496 | tf_op jit(solution)/shard_map/ppermute | solution.py:573
  18.8 0.7 collective-permute-done.4.refs_8_
  19.5 0.2 collective-permute-done.5.refs_9_
  19.8 0.0 collective-permute-done.2.refs_6_
  19.8 0.0 collective-permute-done.3.refs_7_
  19.8 13.4 %products.1 = (f32[16,160,128]{2,1,0:T(8,128)S(1)}, f32[40,128]{1,0:T(8,128)S(1)}) custom-call(f32[16,32,128]{2,1,0:T(8,128)S(1)} %get-tuple-element.21.refs_0_, f32[16,32,128]{2,1,0:T(8,128)S(1)} %get-tuple-element.22.refs_1_, f32[16,8,128]{2,1,0:T(8,128)S(1)} %get-tuple-element.28.refs_2_, f32[16,8,128]{2,1,0:T(8,128)S(1)} %get-tuple-element.29.refs_3_, ...), custom_call_target="tpu_custom_call" | custom-call | tf_op jit(solution)/shard_map/products/pallas_call | solution.py:579
  33.2 6.5 %collective-permute-start.6 = (f32[40,128]{1,0:T(8,128)S(1)}, f32[40,128]{1,0:T(8,128)S(1)}, u32[]{:S(2)}, u32[]{:S(2)}) collective-permute-start(f32[40,128]{1,0:T(8,128)S(1)} %get-tuple-element.36), channel_id=1, source_target_pairs={{0,4},{4,0},{1,5},{5,1},{2,6},{6,2},{3,7},{7,3},{8,12},{12,8},{9,1... | collective-permute-start | bytes 61448 | tf_op jit(solution)/shard_map/ppermute | solution.py:595
  39.7 0.8 %collective-permute-done.6 = f32[40,128]{1,0:T(8,128)S(1)} collective-permute-done((f32[40,128]{1,0:T(8,128)S(1)}, f32[40,128]{1,0:T(8,128)S(1)}, u32[]{:S(2)}, u32[]{:S(2)}) %collective-permute-start.6) | collective-permute-done | bytes 20512 | tf_op jit(solution)/shard_map/ppermute | solution.py:595
  40.6 11.8 %all_to_all.10 = f32[16,40,128]{2,1,0:T(8,128)S(1)} all-to-all(f32[16,40,128]{2,1,0:T(8,128)S(1)} %broadcast_in_dim.4), channel_id=1, replica_groups=mesh['z'=8,'x'=4,'c'=2,'sub'=4] {'x','sub'}, dimensions={0} | all-to-all | bytes 655360 | tf_op jit(solution)/shard_map/all_to_all | solution.py:597
  52.4 16.7 %all_to_all.11.parts = f32[8,40,128]{2,1,0:T(8,128)S(1)} all-to-all(f32[8,40,128]{2,1,0:T(8,128)S(1)} %broadcast_in_dim.5), channel_id=1, replica_groups=mesh['z'=8,'x'=4,'c'=2,'sub'=4] {'z'}, dimensions={0} | all-to-all | bytes 327680 | tf_op jit(solution)/shard_map/all_to_all | solution.py:597
  69.0 6.5 %solve.1 = (f32[512,128]{1,0:T(8,128)}, f32[128,128]{1,0:T(8,128)}) custom-call(f32[8,40,128]{2,1,0:T(8,128)S(1)} %all_to_all.11.parts, f32[16,160,128]{2,1,0:T(8,128)S(1)} %get-tuple-element.37.basis), custom_call_target="tpu_custom_call" | custom-call | tf_op jit(solution)/shard_map/solve/pallas_call | solution.py:600
  (4 shorter events, 0.1 us)
Async XLA Ops:
  3.1 16.7 %collective-permute-start.2 = (f32[784,128]{1,0:T(8,128)S(1)}, f32[784,128]{1,0:T(8,128)S(1)}, u32[]{:S(2)}, u32[]{:S(2)}) collective-permute-start(f32[784,128]{1,0:T(8,128)S(1)} %get-tuple-element.32), channel_id=1, source_target_pairs={{0,4},{4,8},{8,12},{12,16},{16,20},{20,24},{24,28},{28,32},{32,36}... | collective-permute-start | bytes 1204232 | tf_op jit(solution)/shard_map/ppermute | solution.py:563
  5.8 14.0 %collective-permute-start.3 = (f32[784,128]{1,0:T(8,128)S(1)}, f32[784,128]{1,0:T(8,128)S(1)}, u32[]{:S(2)}, u32[]{:S(2)}) collective-permute-start(f32[784,128]{1,0:T(8,128)S(1)} %get-tuple-element.33), channel_id=1, source_target_pairs={{0,252},{4,0},{8,4},{12,8},{16,12},{20,16},{24,20},{28,24},{32,28}... | collective-permute-start | bytes 1204232 | tf_op jit(solution)/shard_map/ppermute | solution.py:562
  6.5 4.6 %collective-permute-start = (f32[176,128]{1,0:T(8,128)S(1)}, f32[176,128]{1,0:T(8,128)S(1)}, u32[]{:S(2)}, u32[]{:S(2)}) collective-permute-start(f32[176,128]{1,0:T(8,128)S(1)} %get-tuple-element.26), channel_id=1, source_target_pairs={{0,1},{1,2},{2,3},{3,0},{4,5},{5,6},{6,7},{7,4},{8,9},{9,10},{10,1... | collective-permute-start | bytes 270344 | tf_op jit(solution)/shard_map/ppermute | solution.py:561
  7.1 4.0 %collective-permute-start.1 = (f32[176,128]{1,0:T(8,128)S(1)}, f32[176,128]{1,0:T(8,128)S(1)}, u32[]{:S(2)}, u32[]{:S(2)}) collective-permute-start(f32[176,128]{1,0:T(8,128)S(1)} %get-tuple-element.27), channel_id=1, source_target_pairs={{0,3},{1,0},{2,1},{3,2},{4,7},{5,4},{6,5},{7,6},{8,11},{9,8},{10,9... | collective-permute-start | bytes 270344 | tf_op jit(solution)/shard_map/ppermute | solution.py:560
  11.3 8.2 %collective-permute-start.4 = (f32[208,128]{1,0:T(8,128)S(1)}, f32[208,128]{1,0:T(8,128)S(1)}, u32[]{:S(2)}, u32[]{:S(2)}) collective-permute-start(f32[208,128]{1,0:T(8,128)S(1)} %get-tuple-element.34), channel_id=1, source_target_pairs={{0,4},{4,8},{8,12},{12,16},{16,20},{20,24},{24,28},{28,32},{32,36}... | collective-permute-start | bytes 319496 | tf_op jit(solution)/shard_map/ppermute | solution.py:574
  14.0 5.8 %collective-permute-start.5 = (f32[208,128]{1,0:T(8,128)S(1)}, f32[208,128]{1,0:T(8,128)S(1)}, u32[]{:S(2)}, u32[]{:S(2)}) collective-permute-start(f32[208,128]{1,0:T(8,128)S(1)} %get-tuple-element.35), channel_id=1, source_target_pairs={{0,252},{4,0},{8,4},{12,8},{16,12},{20,16},{24,20},{28,24},{32,28}... | collective-permute-start | bytes 319496 | tf_op jit(solution)/shard_map/ppermute | solution.py:573
  33.2 7.3 %collective-permute-start.6 = (f32[40,128]{1,0:T(8,128)S(1)}, f32[40,128]{1,0:T(8,128)S(1)}, u32[]{:S(2)}, u32[]{:S(2)}) collective-permute-start(f32[40,128]{1,0:T(8,128)S(1)} %get-tuple-element.36), channel_id=1, source_target_pairs={{0,4},{4,0},{1,5},{5,1},{2,6},{6,2},{3,7},{7,3},{8,12},{12,8},{9,1... | collective-permute-start | bytes 61448 | tf_op jit(solution)/shard_map/ppermute | solution.py:595
